TPU v7x, 32 devices: a whole 2x2x4 slice. The times are simulated.
32 devices in a mesh: blk: 8 (over z, x), grp: 4 (over y, core).
Axes of the slice: x: 2, y: 2, z: 4, core: 2. Of those that a mesh axis runs over, the one named last changes fastest.
Arguments:
- flow: float32 [384, 5, 4096], P(('blk', 'grp')), may hold values from -3 to 6, as said below
- adjoint: float32 [384, 5, 4096], P(('blk', 'grp')), may hold values from -6 to 6
- cut_flag: int32 [384, 4096], P(('blk', 'grp')), may hold values 0 or 1
- lateral_owner: int32 [384, 4, 1], P(('blk', 'grp')), may hold values from 0 to 7; in each aligned block of 48 rows (0 to 47, 48 to 95, ..., all dimensions but the last counted through in order) at most 9 rows name the same one
- lateral_link: int32 [384, 4], P(('blk', 'grp')), may hold values from 0 to 59
- vertical_link: int32 [384, 2], P(('blk', 'grp')), may hold values from 0 to 59
Outputs:
- indicator: float32 [384, 4096], P(('blk', 'grp'))
Inputs may be any that keep to these rules, and one draw needn't show every extreme that they name: `flow`: density lies between 1 and 2, pressure between 1 and 2, every velocity component between -1.25 and 1.25. `lateral_owner`: among the faces 0 to 3 of the blocks of one device, at most 9 have their neighbour on any one blk index, and in every draw some device reaches 9.
All inputs are finite; a program needn't handle non-finite values. No bound on the sum of `cut_flag` on one device may be relied on, other than what follows from the above.
Results may differ from a plain program's by a relative error of at most 0.0003.
Values sent between devices are 32-bit elements; how exact they have to be, the bound alone decides.
A program may use at most 128 MiB of HBM per device.

v0:
```python
import functools

import jax
import jax.numpy as jnp
from jax import lax
from jax.experimental import pallas as pl
from jax.experimental.pallas import tpu as pltpu
from jax.sharding import PartitionSpec as P

EDGE = 16
PLANE = EDGE * EDGE
LANES = 128
PACK = 4
FREESTREAM = (1.0, 0.0, 0.0, 0.3, 1.0)
VMEM = pl.BlockSpec(memory_space=pltpu.VMEM)
SMEM = pl.BlockSpec(memory_space=pltpu.SMEM)
HBM = pl.BlockSpec(memory_space=pltpu.HBM)
MESH = pl.DeviceIdType.MESH


def iota(shape, dim):
    return lax.broadcasted_iota(jnp.int32, shape, dim)


def primitive(state):
    density, mom, energy = state[0], state[1:4], state[4]
    root = lax.rsqrt(density)
    inverse = root * root
    vel = [m * inverse for m in mom]
    square = vel[0] * vel[0] + vel[1] * vel[1] + vel[2] * vel[2]
    return [density, *vel, 0.4 * (energy - 0.5 * density * square)]


def pack_cells(flow_ref, adj_ref, flag_ref, val_ref, solid_ref):
    blocks = flow_ref.shape[1]
    groups = blocks // PACK
    top = iota((8, LANES), 0) < PACK

    def pack(parts):
        tiles = []
        for g in range(groups):
            at = g * PACK % 8
            first, second = parts[g * PACK // 8]
            if first.shape[0] == PACK:
                tiles.append(jnp.concatenate([first, second], axis=0))
            elif at == 0:
                tiles.append(jnp.where(top, first, pltpu.roll(second, 4, 0)))
            else:
                tiles.append(jnp.where(top, pltpu.roll(first, 4, 0), second))
        return tiles

    def read(load, i):
        parts = []
        for start in range(0, blocks, 8):
            rows = slice(start, min(start + 8, blocks))
            parts.append(
                [load(rows, pl.ds(pl.multiple_of(i * PLANE + h * LANES, LANES), LANES)) for h in range(2)]
            )
        return pack(parts)

    def load_layer(i, carry):
        flow = [read(lambda r, s: flow_ref[c, r, s], i) for c in range(5)]
        for g in range(groups):
            for c, x in enumerate(primitive([f[g] for f in flow])):
                val_ref[g, c, i] = x
        for c in range(5):
            for g, x in enumerate(read(lambda r, s: adj_ref[c, r, s], i)):
                val_ref[g, 5 + c, i] = x
        for g, x in enumerate(read(lambda r, s: flag_ref[r, s], i)):
            solid_ref[g, i] = x.astype(jnp.float32)
        return carry

    lax.fori_loop(0, EDGE, load_layer, 0)


def halo_kernel(
    capacity, req_ref, flow_ref, adj_ref, flag_ref, ret_ref, low_ref, high_ref, val_hbm, solid_hbm,
    lat_ref, ver_ref, want_ref, index_ref, stage,
    ask_sem, asked_sem, send_sem, recv_sem, up_sem, down_sem, own_sem, val_ref, solid_ref, pack_sem,
):
    blocks = flow_ref.shape[1]
    peers = req_ref.shape[0]
    me = lax.axis_index("blk")

    def request(d):
        peer = lax.rem(me + d, peers)
        return pltpu.make_async_remote_copy(
            src_ref=req_ref.at[peer],
            dst_ref=want_ref.at[me],
            send_sem=ask_sem.at[d],
            recv_sem=asked_sem.at[d],
            device_id={"blk": peer},
            device_id_type=MESH,
        )

    barrier = pltpu.get_barrier_semaphore()
    for d in range(1, peers):
        pl.semaphore_signal(
            barrier, inc=1, device_id={"blk": lax.rem(me + d, peers)}, device_id_type=MESH
        )
    region = lax.axis_index("grp")
    last = lax.axis_size("grp") - 1
    has_low, has_high = region > 0, region < last
    for there, step in ((has_low, -1), (has_high, 1)):
        @pl.when(there)
        def _():
            pl.semaphore_signal(
                barrier, inc=1, device_id={"grp": region + step}, device_id_type=MESH
            )
    own = pltpu.make_async_copy(req_ref.at[me], want_ref.at[me], own_sem)
    own.start()
    lane = iota((blocks, LANES), 1)
    slot, spot = lane >> 4, lane & 15

    def layers(ref, c):
        def tile(i, half):
            return ref[c, :, i * PLANE + half * LANES : i * PLANE + (half + 1) * LANES]

        out = {}
        for half in range(2):
            out[0, half] = tile(0, half)
            out[1, half] = tile(EDGE - 1, half)
            low_j = high_j = low_k = high_k = jnp.zeros((blocks, LANES), jnp.float32)
            for i in range(EDGE):
                if i // 8 == half:
                    il = i % 8
                    low_j = jnp.where(slot == il, pltpu.roll(tile(i, 0), il * 16, 1), low_j)
                    high_j = jnp.where(
                        slot == il, pltpu.roll(tile(i, 1), (il * 16 + 16) % LANES, 1), high_j
                    )
                here = tile(i, half)
                low_k = jnp.where(spot == i, pltpu.roll(here, i, 1), low_k)
                high_k = jnp.where(spot == i, pltpu.roll(here, (LANES + i - 15) % LANES, 1), high_k)
            out[2, half], out[3, half], out[4, half], out[5, half] = low_j, high_j, low_k, high_k
        return out

    def put(face, half, c, value):
        where = slice(half * LANES, (half + 1) * LANES)
        if face < 4:
            lat_ref[face, c, :, where] = value
        else:
            ver_ref[face - 4, c, :, where] = value

    for c in range(5):
        if c == 3:
            pl.semaphore_wait(
                barrier, peers - 1 + has_low.astype(jnp.int32) + has_high.astype(jnp.int32)
            )
            for d in range(1, peers):
                request(d).start()
        for (face, half), value in layers(flow_ref, c).items():
            put(face, half, c, value)
        for (face, half), value in layers(adj_ref, c).items():
            put(face, half, 5 + c, value)
    for half in range(2):
        where = slice(half * LANES, (half + 1) * LANES)
        for ref, count in ((lat_ref, 4), (ver_ref, 2)):
            for face in range(count):
                prim = primitive([ref[face, c, :, where] for c in range(5)])
                for c in range(1, 5):
                    ref[face, c, :, where] = prim[c]
    own.wait()
    for d in range(1, peers):
        request(d).wait()
    indices = pltpu.make_async_copy(want_ref, index_ref, own_sem)
    indices.start()
    indices.wait()
    def copy(d):
        peer = lax.rem(me + d, peers)
        return pltpu.make_async_remote_copy(
            src_ref=stage.at[peer],
            dst_ref=ret_ref.at[me],
            send_sem=send_sem.at[d],
            recv_sem=recv_sem.at[d],
            device_id={"blk": peer},
            device_id_type=MESH,
        )

    def vertical(source, target, sem, step):
        return pltpu.make_async_remote_copy(
            src_ref=ver_ref.at[source],
            dst_ref=target,
            send_sem=sem.at[0],
            recv_sem=sem.at[1],
            device_id={"grp": region + step},
            device_id_type=MESH,
        )

    upward = vertical(1, low_ref, up_sem, 1)
    downward = vertical(0, high_ref, down_sem, -1)
    def gather(peer, ref, at):
        def one(s, carry):
            code = index_ref[peer, 0, s]
            face, block = code & 3, code >> 2
            for c in range(10):
                ref[at, pl.ds(s * 10 + c, 1), :] = lat_ref[face, c, pl.ds(block, 1), :]
            return carry

        lax.fori_loop(0, capacity, one, 0)

    def fill(d):
        peer = lax.rem(me + d, peers)
        gather(peer, stage, peer)

    fill(1)

    @pl.when(has_high)
    def _():
        upward.start()

    @pl.when(has_low)
    def _():
        downward.start()

    def send(d, carry):
        fill(d)
        copy(d - 1).start()
        return carry

    lax.fori_loop(2, peers, send, 0)
    gather(me, stage, me)
    copy(peers - 1).start()

    def far(ref):
        for c in range(10):
            ref[c] = jnp.full(ref.shape[1:], FREESTREAM[c] if c < 5 else 0.0, jnp.float32)

    mine = pltpu.make_async_copy(stage.at[me], ret_ref.at[me], own_sem)
    mine.start()
    pack_cells(flow_ref, adj_ref, flag_ref, val_ref, solid_ref)

    @pl.when(has_low)
    def _():
        downward.wait_send()
        upward.wait_recv()

    @pl.when(jnp.logical_not(has_low))
    def _():
        far(low_ref)

    @pl.when(has_high)
    def _():
        upward.wait_send()
        downward.wait_recv()

    @pl.when(jnp.logical_not(has_high))
    def _():
        far(high_ref)

    packed = [
        pltpu.make_async_copy(val_ref, val_hbm, pack_sem.at[0]),
        pltpu.make_async_copy(solid_ref, solid_hbm, pack_sem.at[1]),
    ]
    for copy_out in packed:
        copy_out.start()

    def finish(d, carry):
        copy(d).wait()
        return carry

    lax.fori_loop(1, peers, finish, 0)
    mine.wait()
    for copy_out in packed:
        copy_out.wait()


def plan_kernel(capacity, owner_ref, link_ref, req_ref, place_ref, count_ref):
    def clear(p, carry):
        count_ref[p] = 0
        for s in range(capacity):
            req_ref[p, 0, s] = 0
        return carry

    lax.fori_loop(0, req_ref.shape[0], clear, 0)

    def ask(b, carry):
        for f in range(4):
            owner = owner_ref[f, 0, b]
            at = count_ref[owner]
            count_ref[owner] = at + 1
            req_ref[owner, 0, at] = link_ref[f, b] // 5 * 4 + (f ^ 1)
            place_ref[b * 4 + f] = owner * 4096 + at
        return carry

    lax.fori_loop(0, link_ref.shape[1], ask, 0)


def minmod(a, b):
    return jnp.where(a * b > 0.0, jnp.where(jnp.abs(a) < jnp.abs(b), a, b), 0.0)


def derive(state):
    rho, u, v, w, p = state
    inv_root = lax.rsqrt(rho)
    root = rho * inv_root
    enth = (3.5 * p) * (inv_root * inv_root) + 0.5 * (u * u + v * v + w * w)
    return (rho, (u, v, w), p, enth, root, (root * u, root * v, root * w), root * enth)


def roe(left, right, n):
    rho_l, vel_l, p_l, h_l, root_l, rv_l, rh_l = left
    rho_r, vel_r, p_r, h_r, root_r, rv_r, rh_r = right
    t1, t2 = [a for a in range(3) if a != n]
    r = lax.rsqrt(root_l + root_r)
    inv = r * r
    vel = [(a + b) * inv for a, b in zip(rv_l, rv_r)]
    enth = (rh_l + rh_r) * inv
    half_sq = 0.5 * (vel[0] * vel[0] + vel[1] * vel[1] + vel[2] * vel[2])
    c_sq = 0.4 * (enth - half_sq)
    inv_c = lax.rsqrt(c_sq)
    c = c_sq * inv_c
    inv_c_sq = inv_c * inv_c
    rho = root_l * root_r
    un = vel[n]
    dp = p_r - p_l
    scaled = dp * inv_c_sq
    half = 0.5 * scaled
    jump = (0.5 * (rho * inv_c)) * (vel_r[n] - vel_l[n])
    spread, tenth, factor = 0.2 * c, 0.1 * c, 2.5 * inv_c

    def rate(x):
        x = jnp.abs(x)
        return jnp.where(x < spread, x * x * factor + tenth, x)

    slow = rate(un - c) * (half - jump)
    fast = rate(un + c) * (half + jump)
    speed = jnp.abs(un)
    mid = speed * ((rho_r - rho_l) - scaled)
    shear = speed * rho
    both = slow + fast
    diff = c * (fast - slow)
    mass = both + mid
    s1 = shear * (vel_r[t1] - vel_l[t1])
    s2 = shear * (vel_r[t2] - vel_l[t2])
    m_l, m_r = rho_l * vel_l[n], rho_r * vel_r[n]
    out = [None] * 5
    out[0] = m_l + m_r - mass
    out[1 + n] = m_l * vel_l[n] + m_r * vel_r[n] + (p_l + p_r) - (un * mass + diff)
    out[1 + t1] = m_l * vel_l[t1] + m_r * vel_r[t1] - (vel[t1] * mass + s1)
    out[1 + t2] = m_l * vel_l[t2] + m_r * vel_r[t2] - (vel[t2] * mass + s2)
    out[4] = (
        m_l * h_l + m_r * h_r
        - (enth * both + un * diff + mid * half_sq + vel[t1] * s1 + vel[t2] * s2)
    )
    return out


def quads(base, q1, q2):
    low = [b - q for b, q in zip(base, q1)]
    high = [b + q for b, q in zip(base, q1)]
    return [
        derive([b - q for b, q in zip(low, q2)]),
        derive([b + q for b, q in zip(low, q2)]),
        derive([b - q for b, q in zip(high, q2)]),
        derive([b + q for b, q in zip(high, q2)]),
    ]


def moments(lefts, rights, n):
    f = [roe(a, b, n) for a, b in zip(lefts, rights)]
    zero, first, second = [], [], []
    for c in range(5):
        low, high = f[0][c] + f[1][c], f[2][c] + f[3][c]
        zero.append(low + high)
        first.append(high - low)
        second.append((f[1][c] - f[0][c]) + (f[3][c] - f[2][c]))
    return zero + first + second


def dot(a, b):
    total = a[0] * b[0]
    for x, y in zip(a[1:], b[1:]):
        total = total + x * y
    return total


def main_kernel(
    place_ref, link_ref, ver_link_ref,
    ret_hbm, low_hbm, high_hbm, val_hbm, solid_hbm,
    out_ref,
    ret_ref, low_ref, high_ref, sems,
    val, slope, solid, ghost, low_k, low_j, mom_k, mom_j, mom_i, lo_solid,
):
    blocks = link_ref.shape[1]
    groups = blocks // PACK
    lane = iota((8, LANES), 1)
    row = iota((8, LANES), 0)
    top = row < PACK
    slot, spot = lane >> 4, lane & 15

    pairs = ((ret_hbm, ret_ref), (low_hbm, low_ref), (high_hbm, high_ref))
    copies = [pltpu.make_async_copy(a, b, sems.at[at]) for at, (a, b) in enumerate(pairs)]
    inside = pl.ds(1, EDGE)
    cells = [
        pltpu.make_async_copy(val_hbm, val.at[:, :, inside], sems.at[3]),
        pltpu.make_async_copy(solid_hbm, solid.at[:, inside], sems.at[4]),
    ]
    for copy in copies + cells:
        copy.start()
    for copy in copies:
        copy.wait()

    def load_ghost(c, carry):
        for b in range(blocks):
            g, at = b // PACK, b % PACK
            for f in range(6):
                if f < 4:
                    at_row = place_ref[b * 4 + f]
                    x = ret_ref[at_row >> 12, pl.ds((at_row & 4095) * 10 + c, 1), :]
                else:
                    ref = low_ref if f == 4 else high_ref
                    x = ref[c, pl.ds(ver_link_ref[f - 4, b] // 5, 1), :]
                ghost[g, f, c, at : at + 1, :] = x[:, :LANES]
                ghost[g, f, c, PACK + at : PACK + at + 1, :] = x[:, LANES:]
        return carry

    lax.fori_loop(0, 10, load_ghost, 0)
    upper_half = 1 - (row >> 2)
    for g in range(groups):
        for f in range(6):
            code = 0
            for at in range(PACK):
                b = g * PACK + at
                one = lax.rem(link_ref[f, b] if f < 4 else ver_link_ref[f - 4, b], 5)
                if f >= 4:
                    one = jnp.where(one == 4, 4, ((one & 1) << 1) + (one >> 1))
                code = jnp.where((row & 3) == at, one, code)
            half = 1 - upper_half
            own = (code == 4) | ((code >> 1) == half)
            quarter = ((4 * half + (slot >> 1)) << 4) + ((code & 1) << 3) + (spot >> 1)
            index = jnp.where(code == 4, lane, quarter)
            for c in range(10):
                x = ghost[g, f, c]
                x = jnp.where(own, x, pltpu.roll(x, 4, 0))
                x = jnp.take_along_axis(x, index, axis=1, mode="promise_in_bounds")
                ghost[g, f, c] = x
    for g in range(groups):
        nothing = jnp.zeros((8, LANES), jnp.float32)
        solid[g, 0] = nothing
        solid[g, EDGE + 1] = nothing
        for c in range(10):
            val[g, c, 0] = ghost[g, 0, c]
            val[g, c, EDGE + 1] = ghost[g, 1, c]
    for d in range(3):
        for c in range(5):
            nothing = jnp.zeros((8, LANES), jnp.float32)
            slope[d, c, 0] = nothing
            slope[d, c, EDGE + 1] = nothing

    for copy in cells:
        copy.wait()

    def next_k(x, edge, i):
        edge = 0.0 if edge is None else pltpu.roll(edge, 15 - i, 1)
        return jnp.where(spot == 15, edge, pltpu.roll(x, LANES - 1, 1))

    def prev_k(x, edge, i):
        edge = 0.0 if edge is None else pltpu.roll(edge, (LANES - i) % LANES, 1)
        return jnp.where(spot == 0, edge, pltpu.roll(x, 1, 1))

    def place(edge, i, lane_at, upper):
        if edge is None:
            return 0.0
        edge = pltpu.roll(edge, (2 * LANES + lane_at - (i & 7) * 16) % LANES, 1)
        same = (i >> 3) == (1 if upper else 0)
        return jnp.where(same, edge, pltpu.roll(edge, 4, 0))

    def next_j(x, edge, i):
        y = pltpu.roll(x, LANES - 16, 1)
        z = jnp.where(top, pltpu.roll(y, 4, 0), place(edge, i, LANES - 16, True))
        return jnp.where(slot == 7, z, y)

    def prev_j(x, edge, i):
        y = pltpu.roll(x, 16, 1)
        z = jnp.where(top, place(edge, i, 0, False), pltpu.roll(y, 4, 0))
        return jnp.where(slot == 0, z, y)

    def group(g, carry):
        def slopes(i, inner):
            at_k = spot == i
            at_j = ((row >> 2) == (i >> 3)) & (slot == (i & 7))
            for c in range(10):
                own = val[g, c, 1 + i]
                found = [
                    minmod(val[g, c, 2 + i] - own, own - val[g, c, i]),
                    minmod(next_j(own, ghost[g, 3, c], i) - own, own - prev_j(own, ghost[g, 2, c], i)),
                    minmod(next_k(own, ghost[g, 5, c], i) - own, own - prev_k(own, ghost[g, 4, c], i)),
                ]
                found = [0.25 * s for s in found]
                for d in range(3):
                    slope[d, c, 1 + i] = found[d]
                if c < 5:
                    for d, x in enumerate([own, *found]):
                        low_k[d, c] = jnp.where(at_k, pltpu.roll(x, i, 1), low_k[d, c])
                        x = jnp.where(top, x, pltpu.roll(x, 4, 0))
                        low_j[d, c] = jnp.where(at_j, pltpu.roll(x, (i & 7) * 16, 1), low_j[d, c])
            return inner

        lax.fori_loop(0, EDGE, slopes, 0)

        def first_faces(n, lower, cell):
            t1, t2 = [a for a in range(3) if a != n]
            left = derive(lower)
            base = [cell(0, c) - cell(1 + n, c) for c in range(5)]
            rights = quads(base, [cell(1 + t1, c) for c in range(5)], [cell(1 + t2, c) for c in range(5)])
            return moments([left] * 4, rights, n)

        for ref, n in ((mom_j, 1), (mom_k, 2)):
            source = low_j if n == 1 else low_k
            found = first_faces(n, [ghost[g, 2 * n, c] for c in range(5)], lambda d, c: source[d, c])
            for c in range(15):
                ref[c] = found[c]
        found = first_faces(
            0,
            [ghost[g, 0, c] for c in range(5)],
            lambda d, c: val[g, c, 1] if d == 0 else slope[d - 1, c, 1],
        )
        for c in range(15):
            mom_i[c] = found[c]

        def layer(i, inner):
            v = [val[g, c, 1 + i] for c in range(5)]
            q = [[slope[d, c, 1 + i] for c in range(5)] for d in range(3)]
            av = [val[g, 5 + c, 1 + i] for c in range(5)]
            aq = [[slope[d, 5 + c, 1 + i] for c in range(5)] for d in range(3)]
            child = {}
            for a in range(2):
                base = [x + y if a else x - y for x, y in zip(v, q[0])]
                for at, state in enumerate(quads(base, q[1], q[2])):
                    child[a, at >> 1, at & 1] = state

            def side(n, high):
                order = [(s, t) for s in range(2) for t in range(2)]
                return [child[tuple([*st[:n], high, *st[n:]])] for st in order]

            own_solid = solid[g, 1 + i]
            total = jnp.zeros((8, LANES), jnp.float32)
            for n in range(3):
                t1, t2 = [a for a in range(3) if a != n]
                f = [roe(a, b, n) for a, b in zip(side(n, 0), side(n, 1))]
                inside = [(f[0][c] + f[1][c]) + (f[2][c] + f[3][c]) for c in range(5)]
                total = total - 2.0 * dot(aq[n], inside)
                if n == 0:
                    base = [val[g, c, 2 + i] - slope[0, c, 2 + i] for c in range(5)]
                    q1 = [slope[1, c, 2 + i] for c in range(5)]
                    q2 = [slope[2, c, 2 + i] for c in range(5)]
                    up_solid, down_solid = solid[g, 2 + i], solid[g, i]
                else:
                    ahead, behind = (next_j, prev_j) if n == 1 else (next_k, prev_k)
                    base = [ahead(v[c] - q[n][c], ghost[g, 2 * n + 1, c], i) for c in range(5)]
                    q1 = [ahead(q[t1][c], None, i) for c in range(5)]
                    q2 = [ahead(q[t2][c], None, i) for c in range(5)]
                    up_solid, down_solid = ahead(own_solid, None, i), behind(own_solid, None, i)
                above = moments(side(n, 1), quads(base, q1, q2), n)
                if n == 0:
                    below = [mom_i[c] for c in range(15)]
                    for c in range(15):
                        mom_i[c] = above[c]
                else:
                    first = mom_j if n == 1 else mom_k
                    below = [behind(above[c], first[c], i) for c in range(15)]
                outer = [x + y for x, y in zip(av, aq[n])]
                inner_side = [x - y for x, y in zip(av, aq[n])]
                upper = dot([*outer, *aq[t1], *aq[t2]], above)
                lower = dot([*inner_side, *aq[t1], *aq[t2]], below)
                cross = aq[t1][1 + n] * q[t1][4] + aq[t2][1 + n] * q[t2][4]
                wall_up = 8.0 * (outer[1 + n] * (v[4] + q[n][4]) + cross)
                wall_down = 8.0 * (inner_side[1 + n] * (v[4] - q[n][4]) + cross)
                total = total + (
                    jnp.where(up_solid > 0.5, wall_up, upper)
                    - jnp.where(down_solid > 0.5, wall_down, lower)
                )
            total = jnp.where(own_solid > 0.5, 0.0, 0.5 * jnp.abs(total))
            lo_solid[g, i] = total
            return inner

        lax.fori_loop(0, EDGE, layer, 0)
        return carry

    lax.fori_loop(0, groups, group, 0)

    def store(i, carry):
        for g in range(groups):
            x = lo_solid[g, i]
            for h in range(2):
                out_ref[
                    g * PACK : (g + 1) * PACK,
                    pl.ds(pl.multiple_of(i * PLANE + h * LANES, LANES), LANES),
                ] = x[h * PACK : (h + 1) * PACK]
        return carry

    lax.fori_loop(0, EDGE, store, 0)


def local(flow, adjoint, cut_flag, lateral_owner, lateral_link, vertical_link):
    blocks = flow.shape[0]
    groups = blocks // PACK
    peers = lax.axis_size("blk")
    capacity = max(2, 6 * blocks // peers)
    flow_t = jnp.transpose(flow, (1, 0, 2))
    adj_t = jnp.transpose(adjoint, (1, 0, 2))
    f32 = functools.partial(jax.ShapeDtypeStruct, dtype=jnp.float32)

    owner_t = jnp.transpose(lateral_owner, (1, 2, 0))
    link_t, ver_link_t = lateral_link.T, vertical_link.T
    i32 = functools.partial(jax.ShapeDtypeStruct, dtype=jnp.int32)
    requests, place = pl.pallas_call(
        functools.partial(plan_kernel, capacity),
        out_shape=(i32((peers, 1, LANES)), i32((blocks * 4,))),
        in_specs=[SMEM, SMEM],
        out_specs=(SMEM, SMEM),
        scratch_shapes=[pltpu.SMEM((peers,), jnp.int32)],
        name="plan",
    )(owner_t, link_t)

    received = (peers, capacity * 10, PLANE)
    cells = (groups, 10, EDGE, 8, LANES)
    flags = (groups, EDGE, 8, LANES)
    returned, from_low, from_high, packed, solid = pl.pallas_call(
        functools.partial(halo_kernel, capacity),
        out_shape=(
            f32(received),
            f32((10, blocks, PLANE)),
            f32((10, blocks, PLANE)),
            f32(cells),
            f32(flags),
        ),
        in_specs=[VMEM] * 4,
        out_specs=(HBM, VMEM, VMEM, HBM, HBM),
        scratch_shapes=[
            pltpu.VMEM((4, 10, blocks, PLANE), jnp.float32),
            pltpu.VMEM((2, 10, blocks, PLANE), jnp.float32),
            pltpu.VMEM((peers, 1, LANES), jnp.int32),
            pltpu.SMEM((peers, 1, LANES), jnp.int32),
            pltpu.VMEM(received, jnp.float32),
            *[pltpu.SemaphoreType.DMA((peers,))] * 4,
            pltpu.SemaphoreType.DMA((2,)),
            pltpu.SemaphoreType.DMA((2,)),
            pltpu.SemaphoreType.DMA,
            pltpu.VMEM(cells, jnp.float32),
            pltpu.VMEM(flags, jnp.float32),
            pltpu.SemaphoreType.DMA((2,)),
        ],
        compiler_params=pltpu.CompilerParams(collective_id=0, has_side_effects=True),
        name="halo",
    )(requests, flow_t, adj_t, cut_flag)

    tile = functools.partial(pltpu.VMEM, dtype=jnp.float32)
    return pl.pallas_call(
        main_kernel,
        out_shape=f32((blocks, EDGE * PLANE)),
        in_specs=[SMEM] * 3 + [HBM] * 5,
        out_specs=VMEM,
        scratch_shapes=[
            tile(received),
            tile((10, blocks, PLANE)),
            tile((10, blocks, PLANE)),
            pltpu.SemaphoreType.DMA((5,)),
            tile((groups, 10, EDGE + 2, 8, LANES)),
            tile((3, 10, EDGE + 2, 8, LANES)),
            tile((groups, EDGE + 2, 8, LANES)),
            tile((groups, 6, 10, 8, LANES)),
            tile((4, 5, 8, LANES)),
            tile((4, 5, 8, LANES)),
            tile((15, 8, LANES)),
            tile((15, 8, LANES)),
            tile((15, 8, LANES)),
            tile((groups, EDGE, 8, LANES)),
        ],
        compiler_params=pltpu.CompilerParams(vmem_limit_bytes=63 * 1024 * 1024),
        name="indicator",
    )(
        place, link_t, ver_link_t,
        returned, from_low, from_high, packed, solid,
    )


def solution(mesh):
    spec3 = P(("blk", "grp"), None, None)
    spec2 = P(("blk", "grp"), None)
    return jax.shard_map(
        local,
        mesh=mesh,
        in_specs=(spec3, spec3, spec2, spec3, spec2, spec2),
        out_specs=spec2,
        check_vma=False,
    )
```

profile of v0, /device:TPU:14, one launch (start us, length us, event | category | flops | bytes accessed | tf_op | source)
XLA Modules:
  0.0 77.5 jit_solution(13633413059279373300)
XLA Ops:
  0.0 2.0 %plan.1 = (s32[8,1,128]{2,1,0:T(1,128)}, s32[48]{0:T(128)}) custom-call(s32[4,1,12]{2,1,0:T(1,128)} %bitcast.9, s32[4,12]{1,0:T(4,128)} %bitcast.7), custom_call_target="tpu_custom_call" | custom-call | tf_op jit(solution)/shard_map/plan/pallas_call | solution.py:607
  2.0 29.3 %halo.1 = (f32[8,90,256]{2,1,0:T(8,128)}, f32[10,12,256]{2,1,0:T(8,128)}, f32[10,12,256]{2,1,0:T(8,128)}, f32[3,10,16,8,128]{4,3,2,1,0:T(8,128)}, f32[3,16,8,128]{3,2,1,0:T(8,128)}) custom-call(s32[8,1,128]{2,1,0:T(1,128)} %get-tuple-element.13.req_ref, f32[5,12,4096]{2,1,0:T(8,128)} %bitcast.5, f32[5,12,4096]{2,1,0:T(8,128)} %bitcast.6, s32[12,4096]{1,0:T(8,128)} %flag_ref.1), custom_call_target="tpu_custom_call" | custom-call | tf_op jit(solution)/shard_map/halo/pallas_call | solution.py:619
  31.3 46.2 %indicator.1 = f32[12,4096]{1,0:T(8,128)} custom-call(s32[48]{0:T(128)} %get-tuple-element.12.place_ref, s32[4,12]{1,0:T(4,128)} %bitcast.8, s32[2,12]{1,0:T(2,128)} %bitcast.10, f32[8,90,256]{2,1,0:T(8,128)} %get-tuple-element.14.ret_hbm, f32[10,12,256]{2,1,0:T(8,128)} %get-tuple-element.15.low_hbm, f32[10,12,256]{2,1,0:T(8,128)} %get-tuple-element.16.high_hbm, ...), custom_call_target="tpu_custom_call" | custom-call | tf_op jit(solution)/shard_map/indicator/pallas_call | solution.py:649
where the time goes:
time: 77.7 us; the launch traced here: 77.5 us
  Pallas kernels  77.5 us (100%)
    pallas_call x1, Pallas kernels, local(): pl.pallas_call(main_kernel, out_shape=f32((blocks, EDGE * PLANE)), in_spe...  46.2 us
    pallas_call x1, Pallas kernels, local(): pl.pallas_call(functools.partial(halo_kernel, capacity), out_shape=(f32(r...  29.3 us
    pallas_call x1, Pallas kernels, local(): pl.pallas_call(functools.partial(plan_kernel, capacity), out_shape=(i32((...  1.96 us

commit v1 on v0

v1 whole, which is shorter than its diff:
```python
import functools

import jax
import jax.numpy as jnp
from jax import lax
from jax.experimental import pallas as pl
from jax.experimental.pallas import tpu as pltpu
from jax.sharding import PartitionSpec as P

EDGE = 16
PLANE = EDGE * EDGE
LANES = 128
PACK = 4
FREESTREAM = (1.0, 0.0, 0.0, 0.3, 1.0)
VMEM = pl.BlockSpec(memory_space=pltpu.VMEM)
SMEM = pl.BlockSpec(memory_space=pltpu.SMEM)
HBM = pl.BlockSpec(memory_space=pltpu.HBM)
MESH = pl.DeviceIdType.MESH


def iota(shape, dim):
    return lax.broadcasted_iota(jnp.int32, shape, dim)


def primitive(state):
    density, mom, energy = state[0], state[1:4], state[4]
    root = lax.rsqrt(density)
    inverse = root * root
    vel = [m * inverse for m in mom]
    square = vel[0] * vel[0] + vel[1] * vel[1] + vel[2] * vel[2]
    return [density, *vel, 0.4 * (energy - 0.5 * density * square)]


def pack_cells(flow_ref, adj_ref, flag_ref, val_ref, solid_ref):
    blocks = flow_ref.shape[1]
    groups = blocks // PACK
    top = iota((8, LANES), 0) < PACK

    def pack(parts):
        tiles = []
        for g in range(groups):
            at = g * PACK % 8
            first, second = parts[g * PACK // 8]
            if first.shape[0] == PACK:
                tiles.append(jnp.concatenate([first, second], axis=0))
            elif at == 0:
                tiles.append(jnp.where(top, first, pltpu.roll(second, 4, 0)))
            else:
                tiles.append(jnp.where(top, pltpu.roll(first, 4, 0), second))
        return tiles

    def read(load, i):
        parts = []
        for start in range(0, blocks, 8):
            rows = slice(start, min(start + 8, blocks))
            parts.append(
                [load(rows, pl.ds(pl.multiple_of(i * PLANE + h * LANES, LANES), LANES)) for h in range(2)]
            )
        return pack(parts)

    def load_layer(i, carry):
        flow = [read(lambda r, s: flow_ref[c, r, s], i) for c in range(5)]
        for g in range(groups):
            for c, x in enumerate(primitive([f[g] for f in flow])):
                val_ref[g, c, i] = x
        for c in range(5):
            for g, x in enumerate(read(lambda r, s: adj_ref[c, r, s], i)):
                val_ref[g, 5 + c, i] = x
        for g, x in enumerate(read(lambda r, s: flag_ref[r, s], i)):
            solid_ref[g, i] = x.astype(jnp.float32)
        return carry

    lax.fori_loop(0, EDGE, load_layer, 0)


def minmod(a, b):
    return jnp.where(a * b > 0.0, jnp.where(jnp.abs(a) < jnp.abs(b), a, b), 0.0)


def halo_kernel(
    capacity, owner_ref, link_ref, ver_link_ref, flow_hbm, adj_hbm, flag_hbm,
    ret_ref, val_hbm, slope_hbm, solid_hbm, kghost_ref, edge_hbm,
    flow_ref, adj_ref, flag_ref, lat_ref, ver_ref, req_ref, want_ref, index_ref, stage, low_ref, high_ref,
    val, slope, solid_ref, edge,
    ask_sem, asked_sem, send_sem, recv_sem, up_sem, down_sem, own_sem, in_sem, pack_sem,
):
    blocks = flow_ref.shape[1]
    groups = blocks // PACK
    peers = req_ref.shape[0]
    rows = stage.shape[1]
    me = lax.axis_index("blk")
    region = lax.axis_index("grp")
    last = lax.axis_size("grp") - 1
    has_low, has_high = region > 0, region < last

    barrier = pltpu.get_barrier_semaphore()
    for d in range(1, peers):
        pl.semaphore_signal(
            barrier, inc=1, device_id={"blk": lax.rem(me + d, peers)}, device_id_type=MESH
        )
    for there, step in ((has_low, -1), (has_high, 1)):
        @pl.when(there)
        def _():
            pl.semaphore_signal(
                barrier, inc=1, device_id={"grp": region + step}, device_id_type=MESH
            )

    loads = [
        pltpu.make_async_copy(a, b, in_sem.at[at])
        for at, (a, b) in enumerate(((flow_hbm, flow_ref), (adj_hbm, adj_ref), (flag_hbm, flag_ref)))
    ]
    for load in loads:
        load.start()

    holder = iota((peers, LANES), 0)
    column = iota((peers, LANES), 1)

    def ask(b, carry):
        asked, count = carry
        for f in range(4):
            code = link_ref[f, b] // 5 * 4 + (f ^ 1)
            match = holder == owner_ref[f, 0, b]
            asked = jnp.where(match & (column == count), code, asked)
            count = count + match.astype(jnp.int32)
        return asked, count

    nobody = jnp.zeros((peers, LANES), jnp.int32)
    asked, _ = lax.fori_loop(0, blocks, ask, (nobody, nobody))
    for p in range(peers):
        req_ref[p] = asked[p : p + 1]

    def request(d):
        peer = lax.rem(me + d, peers)
        return pltpu.make_async_remote_copy(
            src_ref=req_ref.at[peer],
            dst_ref=want_ref.at[me],
            send_sem=ask_sem.at[d],
            recv_sem=asked_sem.at[d],
            device_id={"blk": peer},
            device_id_type=MESH,
        )

    own = pltpu.make_async_copy(req_ref.at[me], want_ref.at[me], own_sem)
    own.start()
    lane = iota((blocks, LANES), 1)
    slot, spot = lane >> 4, lane & 15

    def layers(ref, c):
        def tile(i, half):
            return ref[c, :, i * PLANE + half * LANES : i * PLANE + (half + 1) * LANES]

        out = {}
        for half in range(2):
            out[0, half] = tile(0, half)
            out[1, half] = tile(EDGE - 1, half)
            low_j = high_j = low_k = high_k = jnp.zeros((blocks, LANES), jnp.float32)
            for i in range(EDGE):
                if i // 8 == half:
                    il = i % 8
                    low_j = jnp.where(slot == il, pltpu.roll(tile(i, 0), il * 16, 1), low_j)
                    high_j = jnp.where(
                        slot == il, pltpu.roll(tile(i, 1), (il * 16 + 16) % LANES, 1), high_j
                    )
                here = tile(i, half)
                low_k = jnp.where(spot == i, pltpu.roll(here, i, 1), low_k)
                high_k = jnp.where(spot == i, pltpu.roll(here, (LANES + i - 15) % LANES, 1), high_k)
            out[2, half], out[3, half], out[4, half], out[5, half] = low_j, high_j, low_k, high_k
        return out

    def put(face, half, c, value):
        where = slice(half * LANES, (half + 1) * LANES)
        if face < 4:
            lat_ref[face, c, :, where] = value
        else:
            ver_ref[face - 4, c, :, where] = value

    loads[0].wait()
    loads[1].wait()
    for c in range(5):
        if c == 2:
            pl.semaphore_wait(
                barrier, peers - 1 + has_low.astype(jnp.int32) + has_high.astype(jnp.int32)
            )
            for d in range(1, peers):
                request(d).start()
        for (face, half), value in layers(flow_ref, c).items():
            put(face, half, c, value)
        for (face, half), value in layers(adj_ref, c).items():
            put(face, half, 5 + c, value)
    for half in range(2):
        where = slice(half * LANES, (half + 1) * LANES)
        for ref, count in ((ver_ref, 2), (lat_ref, 4)):
            for face in range(count):
                prim = primitive([ref[face, c, :, where] for c in range(5)])
                for c in range(1, 5):
                    ref[face, c, :, where] = prim[c]

    def vertical(source, target, sem, step):
        return pltpu.make_async_remote_copy(
            src_ref=ver_ref.at[source],
            dst_ref=target,
            send_sem=sem.at[0],
            recv_sem=sem.at[1],
            device_id={"grp": region + step},
            device_id_type=MESH,
        )

    upward = vertical(1, low_ref, up_sem, 1)
    downward = vertical(0, high_ref, down_sem, -1)

    @pl.when(has_high)
    def _():
        upward.start()

    @pl.when(has_low)
    def _():
        downward.start()

    loads[2].wait()
    pack_cells(flow_ref, adj_ref, flag_ref, val, solid_ref)

    own.wait()
    for d in range(1, peers):
        request(d).wait()
    indices = pltpu.make_async_copy(want_ref, index_ref, own_sem)
    indices.start()
    indices.wait()

    def copy(d):
        peer = lax.rem(me + d, peers)
        return pltpu.make_async_remote_copy(
            src_ref=stage.at[peer],
            dst_ref=ret_ref.at[me],
            send_sem=send_sem.at[d],
            recv_sem=recv_sem.at[d],
            device_id={"blk": peer},
            device_id_type=MESH,
        )

    def gather(peer):
        def one(s, carry):
            code = index_ref[peer, 0, s]
            face, block = code & 3, code >> 2
            for c in range(10):
                x = lat_ref[face, c, pl.ds(block, 1), :]
                for h in range(2):
                    stage[peer, pl.ds(s * 20 + c * 2 + h, 1), :] = x[:, h * LANES : (h + 1) * LANES]
            return carry

        lax.fori_loop(0, capacity, one, 0)

    def send(t, carry):
        sign = 2 * lax.rem(t, 2) - 1
        d = peers // 2 + (t + 1) // 2 * sign
        gather(lax.rem(me + d, peers))
        copy(d).start()
        return carry

    lax.fori_loop(0, peers - 1, send, 0)
    gather(me)
    mine = pltpu.make_async_copy(stage.at[me], ret_ref.at[me], own_sem)
    mine.start()

    packed = [
        pltpu.make_async_copy(val, val_hbm, pack_sem.at[0]),
        pltpu.make_async_copy(solid_ref, solid_hbm, pack_sem.at[1]),
    ]
    for copy_out in packed:
        copy_out.start()

    def far(ref):
        for c in range(10):
            ref[c] = jnp.full(ref.shape[1:], FREESTREAM[c] if c < 5 else 0.0, jnp.float32)

    @pl.when(has_low)
    def _():
        downward.wait_send()
        upward.wait_recv()

    @pl.when(jnp.logical_not(has_low))
    def _():
        far(low_ref)

    @pl.when(has_high)
    def _():
        upward.wait_send()
        downward.wait_recv()

    @pl.when(jnp.logical_not(has_high))
    def _():
        far(high_ref)

    lane = iota((8, LANES), 1)
    row = iota((8, LANES), 0)
    top = row < PACK
    slot, spot = lane >> 4, lane & 15

    def load_ghost(c, carry):
        for b in range(blocks):
            g, at = b // PACK, b % PACK
            for f, ref in enumerate((low_ref, high_ref)):
                x = ref[c, pl.ds(ver_link_ref[f, b] // 5, 1), :]
                kghost_ref[g, f, c, at : at + 1, :] = x[:, :LANES]
                kghost_ref[g, f, c, PACK + at : PACK + at + 1, :] = x[:, LANES:]
        return carry

    lax.fori_loop(0, 10, load_ghost, 0)
    half = row >> 2
    for g in range(groups):
        for f in range(2):
            code = jnp.zeros((8, LANES), jnp.int32)
            for at in range(PACK):
                one = lax.rem(ver_link_ref[f, g * PACK + at], 5)
                one = jnp.where(one == 4, 4, ((one & 1) << 1) + (one >> 1))
                code = jnp.where((row & 3) == at, one, code)
            mine_half = (code == 4) | ((code >> 1) == half)
            quarter = ((4 * half + (slot >> 1)) << 4) + ((code & 1) << 3) + (spot >> 1)
            index = jnp.where(code == 4, lane, quarter)
            for c in range(10):
                x = kghost_ref[g, f, c]
                x = jnp.where(mine_half, x, pltpu.roll(x, 4, 0))
                x = jnp.take_along_axis(x, index, axis=1, mode="promise_in_bounds")
                kghost_ref[g, f, c] = x

    def slopes_of(g, carry):
        def slopes(i, inner):
            below, above = jnp.maximum(i - 1, 0), jnp.minimum(i + 1, EDGE - 1)
            turn = (i & 7) * 16
            held = slot == jnp.where(top, i & 7, (i + 7) & 7)
            for c in range(10):
                own = val[g, c, i]
                y = pltpu.roll(own, LANES - 16, 1)
                next_j = jnp.where(slot == 7, pltpu.roll(y, 4, 0), y)
                y = pltpu.roll(own, 16, 1)
                prev_j = jnp.where(slot == 0, pltpu.roll(y, 4, 0), y)
                next_k = jnp.where(
                    spot == 15,
                    pltpu.roll(kghost_ref[g, 1, c], 15 - i, 1),
                    pltpu.roll(own, LANES - 1, 1),
                )
                prev_k = jnp.where(
                    spot == 0,
                    pltpu.roll(kghost_ref[g, 0, c], lax.rem(LANES - i, LANES), 1),
                    pltpu.roll(own, 1, 1),
                )
                up, down = next_j - own, own - prev_j
                slope[g, 0, c, i] = 0.25 * minmod(val[g, c, above] - own, own - val[g, c, below])
                slope[g, 1, c, i] = 0.25 * minmod(up, down)
                slope[g, 2, c, i] = 0.25 * minmod(next_k - own, own - prev_k)
                inside = pltpu.roll(jnp.where(top, up, down), turn, 1)
                edge[g, 0, c, i >> 3] = jnp.where(held, inside, edge[g, 0, c, i >> 3])
                edge[g, 1, c, i >> 3] = jnp.where(held, pltpu.roll(own, turn, 1), edge[g, 1, c, i >> 3])
            return inner

        for at in range(2):
            for c in range(10):
                for p in range(2):
                    edge[g, at, c, p] = jnp.zeros((8, LANES), jnp.float32)
        lax.fori_loop(0, EDGE, slopes, 0)
        out(g).start()
        return carry

    def out(g):
        return pltpu.make_async_copy(slope.at[g], slope_hbm.at[g], pack_sem.at[3 + g])

    lax.fori_loop(0, groups, slopes_of, 0)
    edges = pltpu.make_async_copy(edge, edge_hbm, pack_sem.at[2])
    edges.start()

    def finish(d, carry):
        copy(d).wait()
        return carry

    lax.fori_loop(1, peers, finish, 0)
    mine.wait()
    for copy_out in packed:
        copy_out.wait()
    edges.wait()
    for g in range(groups):
        out(g).wait()


def basic(state):
    rho, u, v, w, p = state
    inv_root = lax.rsqrt(rho)
    root = rho * inv_root
    enth = (3.5 * p) * (inv_root * inv_root) + 0.5 * (u * u + v * v + w * w)
    return [root, u, v, w, p, enth]


def full(parts):
    root, u, v, w, p, enth = parts
    return (root, (u, v, w), p, enth, (root * u, root * v, root * w), root * enth)


def roe(left, right, n):
    root_l, vel_l, p_l, h_l, rv_l, rh_l = left
    root_r, vel_r, p_r, h_r, rv_r, rh_r = right
    r = lax.rsqrt(root_l + root_r)
    inv = r * r
    vel = [(a + b) * inv for a, b in zip(rv_l, rv_r)]
    enth = (rh_l + rh_r) * inv
    un = vel[n]
    c_sq = 0.4 * enth - 0.2 * (vel[0] * vel[0] + vel[1] * vel[1] + vel[2] * vel[2])
    inv_c = lax.rsqrt(c_sq)
    c = c_sq * inv_c
    speed = jnp.abs(un)
    mach = speed * inv_c
    t = 1.0 - mach
    z = jnp.maximum(0.2 - jnp.abs(t), 0.0)
    w = (1.25 * z) * z
    even = jnp.maximum(t, 0.0) + w
    odd = jnp.minimum(mach, 1.0) - w
    odd = jnp.where(un < 0.0, -odd, odd)
    dp = p_r - p_l
    a = dp * inv_c
    b = (root_l * root_r) * (vel_r[n] - vel_l[n])
    first = (even * a + odd * b) * inv
    second = c * (odd * a + even * b)
    m_l = root_l * (root_l * (vel_l[n] + speed) - first)
    m_r = root_r * (root_r * (vel_r[n] - speed) - first)
    out = [m_l + m_r] + [m_l * x + m_r * y for x, y in zip(vel_l, vel_r)]
    out[1 + n] = out[1 + n] + ((p_l + p_r) - second)
    out.append((m_l * h_l + m_r * h_r) + (speed * dp - second * un))
    return out


def quads(base, q1, q2):
    low = [b - q for b, q in zip(base, q1)]
    high = [b + q for b, q in zip(base, q1)]
    return [
        basic([b - q for b, q in zip(low, q2)]),
        basic([b + q for b, q in zip(low, q2)]),
        basic([b - q for b, q in zip(high, q2)]),
        basic([b + q for b, q in zip(high, q2)]),
    ]


def moments(lefts, rights, n):
    f = [roe(a, b, n) for a, b in zip(lefts, rights)]
    zero, first, second = [], [], []
    for c in range(5):
        low, high = f[0][c] + f[1][c], f[2][c] + f[3][c]
        zero.append(low + high)
        first.append(high - low)
        second.append((f[1][c] - f[0][c]) + (f[3][c] - f[2][c]))
    return zero + first + second


def dot(a, b):
    total = a[0] * b[0]
    for x, y in zip(a[1:], b[1:]):
        total = total + x * y
    return total


def main_kernel(
    owner_ref, link_ref,
    ret_hbm, kghost_hbm, val_hbm, slope_hbm, solid_hbm, edge_hbm,
    out_ref,
    ret_ref, kghost, val, slope, solid, edge, sems, place_ref, count_ref,
    raw_i, raw_j, fixed, jedge, kedge, carry_hi, carry_sum, first_k, first_j, start_k, start_j, total_ref, found_ref,
):
    blocks = link_ref.shape[1]
    groups = blocks // PACK
    peers = count_ref.shape[0]
    rows = ret_ref.shape[0] // peers
    lane = iota((8, LANES), 1)
    row = iota((8, LANES), 0)
    top = row < PACK
    slot, spot = lane >> 4, lane & 15
    nothing = jnp.zeros((8, LANES), jnp.float32)

    returned = pltpu.make_async_copy(ret_hbm, ret_ref, sems.at[0])
    returned.start()
    shared = [
        pltpu.make_async_copy(kghost_hbm, kghost, sems.at[1]),
        pltpu.make_async_copy(solid_hbm, solid.at[:, pl.ds(1, EDGE)], sems.at[2]),
        pltpu.make_async_copy(edge_hbm, edge, sems.at[3]),
    ]
    for copy in shared:
        copy.start()

    def cells(g):
        return (
            pltpu.make_async_copy(val_hbm.at[g], val.at[g], sems.at[4 + 2 * g]),
            pltpu.make_async_copy(slope_hbm.at[g], slope.at[g], sems.at[5 + 2 * g]),
        )

    for g in range(groups):
        for copy in cells(g):
            copy.start()

    def clear(p, carry):
        count_ref[p] = 0
        return carry

    lax.fori_loop(0, peers, clear, 0)

    def plan(b, carry):
        for f in range(4):
            owner = owner_ref[f, 0, b]
            at = count_ref[owner]
            count_ref[owner] = at + 1
            place_ref[b * 4 + f] = owner * rows + at * 20
        return carry

    lax.fori_loop(0, blocks, plan, 0)
    returned.wait()

    def load_ghost(b, carry):
        g, at = b // PACK, lax.rem(b, PACK)
        for f in range(4):
            code = lax.rem(link_ref[f, b], 5)
            base = place_ref[b * 4 + f]
            for h in range(2):
                from_row = base + jnp.where(code == 4, h, code >> 1)
                for c in range(10):
                    x = ret_ref[pl.ds(from_row + 2 * c, 1), :]
                    if f < 2:
                        raw_i[g, f, c, pl.ds(h * PACK + at, 1), :] = x
                    else:
                        raw_j[g, c, h, pl.ds((f - 2) * PACK + at, 1), :] = x
        return carry

    lax.fori_loop(0, blocks, load_ghost, 0)

    def codes(g, face_of_half):
        code = jnp.zeros((8, LANES), jnp.int32)
        for r in range(8):
            one = lax.rem(link_ref[face_of_half[r // PACK], g * PACK + r % PACK], 5)
            code = jnp.where(row == r, one, code)
        return code

    def picks(code, half, at):
        quarter = ((4 * half + (at >> 1)) << 4) + ((code & 1) << 3) + (spot >> 1)
        return jnp.where(code == 4, at * 16 + spot, quarter)

    def pick(x, index):
        return jnp.take_along_axis(x, index, axis=1, mode="promise_in_bounds")

    for g in range(groups):
        for f in range(2):
            index = picks(codes(g, (f, f)), row >> 2, slot)
            for c in range(10):
                raw_i[g, f, c] = pick(raw_i[g, f, c], index)
        code = codes(g, (2, 3))
        for p in range(2):
            index = picks(code, p, jnp.where(top, slot, (slot + 1) & 7))
            for c in range(10):
                raw_j[g, c, p] = pick(raw_j[g, c, p], index)
        solid[g, 0] = nothing
        solid[g, EDGE + 1] = nothing
    for copy in shared:
        copy.wait()

    def next_k(x):
        return pltpu.roll(x, LANES - 1, 1)

    def prev_k(x):
        return pltpu.roll(x, 1, 1)

    def next_j(x, edge_x):
        y = pltpu.roll(x, LANES - 16, 1)
        z = pltpu.roll(y, 4, 0)
        if edge_x is not None:
            z = jnp.where(top, z, edge_x)
        return jnp.where(slot == 7, z, y)

    def prev_j(x):
        y = pltpu.roll(x, 16, 1)
        return jnp.where(slot == 0, pltpu.roll(y, 4, 0), y)

    last_j = (slot == 7) & jnp.logical_not(top)
    zero_j = (slot == 0) & top
    rim_j = last_j | zero_j

    def group(g, carry):
        for copy in cells(g):
            copy.wait()
        for c in range(10):
            for p in range(2):
                own, ghost = edge[g, 1, c, p], raw_j[g, c, p]
                other = jnp.where(top, own - ghost, ghost - own)
                fixed[c, p] = 0.25 * minmod(edge[g, 0, c, p], other)
            first, second = val[g, c, 0], val[g, c, 1]
            slope[g, 0, c, 0] = 0.25 * minmod(second - first, first - raw_i[g, 0, c])
            first, second = val[g, c, EDGE - 2], val[g, c, EDGE - 1]
            slope[g, 0, c, EDGE - 1] = 0.25 * minmod(raw_i[g, 1, c] - second, second - first)
        for p in range(2):
            for at, x in enumerate(basic([raw_j[g, c, p] for c in range(5)])):
                jedge[at, p] = x
        for at, x in enumerate(basic([kghost[g, 1, c] for c in range(5)])):
            kedge[at] = x
        for at, x in enumerate(basic([raw_i[g, 0, c] for c in range(5)])):
            for s in range(4):
                carry_hi[s, at] = x
        carry_sum[0] = nothing
        carry_sum[1] = nothing

        def join(at, lefts, rights):
            f = moments(lefts, rights, 0)
            below = jnp.maximum(at - 1, 0)
            outer = [val[g, 5 + c, below] + slope[g, 0, 5 + c, below] for c in range(5)]
            aq1 = [slope[g, 1, 5 + c, below] for c in range(5)]
            aq2 = [slope[g, 2, 5 + c, below] for c in range(5)]
            return f, outer, aq1, aq2

        def layer(i, inner):
            turn = lax.rem(LANES - (i & 7) * 16, LANES)
            v = [val[g, c, i] for c in range(5)]
            av = [val[g, 5 + c, i] for c in range(5)]
            q = [[slope[g, d, c, i] for c in range(5)] for d in range(3)]
            aq = [[slope[g, d, 5 + c, i] for c in range(5)] for d in range(3)]
            for c in range(5):
                q[1][c] = jnp.where(rim_j, pltpu.roll(fixed[c, i >> 3], turn, 1), q[1][c])
                aq[1][c] = jnp.where(rim_j, pltpu.roll(fixed[5 + c, i >> 3], turn, 1), aq[1][c])
                slope[g, 1, 5 + c, i] = aq[1][c]
            child, part = {}, {}
            for a in range(2):
                base = [x + y if a else x - y for x, y in zip(v, q[0])]
                for at, state in enumerate(quads(base, q[1], q[2])):
                    part[a, at >> 1, at & 1] = state
                    child[a, at >> 1, at & 1] = full(state)

            def side(store, n, high):
                order = [(s, t) for s in range(2) for t in range(2)]
                return [store[tuple([*st[:n], high, *st[n:]])] for st in order]

            own_solid = solid[g, 1 + i]
            total = nothing
            wall_above = nothing
            for n in range(3):
                t1, t2 = [a for a in range(3) if a != n]
                f = [roe(a, b, n) for a, b in zip(side(child, n, 0), side(child, n, 1))]
                inside = [(f[0][c] + f[1][c]) + (f[2][c] + f[3][c]) for c in range(5)]
                total = total - 2.0 * dot(aq[n], inside)
                outer = [x + y for x, y in zip(av, aq[n])]
                inner_side = [x - y for x, y in zip(av, aq[n])]
                cross = aq[t1][1 + n] * q[t1][4] + aq[t2][1 + n] * q[t2][4]
                wall_up = 8.0 * (outer[1 + n] * (v[4] + q[n][4]) + cross)
                wall_down = 8.0 * (inner_side[1 + n] * (v[4] - q[n][4]) + cross)
                if n == 0:
                    lefts = [full([carry_hi[s, at] for at in range(6)]) for s in range(4)]
                    below, before, b1, b2 = join(i, lefts, side(child, 0, 0))
                    for s, state in enumerate(side(part, 0, 1)):
                        for at in range(6):
                            carry_hi[s, at] = state[at]
                    ahead = dot([*before, *b1, *b2], below)
                    total_ref[i] = carry_sum[0] + jnp.where(own_solid > 0.5, carry_sum[1], ahead)
                    lower = dot([*inner_side, *aq[1], *aq[2]], below)
                    total = total - jnp.where(solid[g, i] > 0.5, wall_down, lower)
                    wall_above = wall_up
                    continue
                if n == 1:
                    rims = [pltpu.roll(jedge[at, i >> 3], turn, 1) for at in range(6)]
                    rights = [
                        full([next_j(x, rim) for x, rim in zip(state, rims)]) for state in side(part, 1, 0)
                    ]
                    above = moments(side(child, 1, 1), rights, 1)
                    below = [prev_j(x) for x in above]
                    up_solid = jnp.where(last_j, 0.0, next_j(own_solid, None))
                    down_solid = prev_j(own_solid)
                    rim = zero_j
                else:
                    rims = [pltpu.roll(kedge[at], 15 - i, 1) for at in range(6)]
                    rights = [
                        full([jnp.where(spot == 15, rim, next_k(x)) for x, rim in zip(state, rims)])
                        for state in side(part, 2, 0)
                    ]
                    above = moments(side(child, 2, 1), rights, 2)
                    below = [prev_k(x) for x in above]
                    up_solid = jnp.where(spot == 15, 0.0, next_k(own_solid))
                    down_solid = prev_k(own_solid)
                    rim = spot == 0
                upper = dot([*outer, *aq[t1], *aq[t2]], above)
                lower = dot([*inner_side, *aq[t1], *aq[t2]], below)
                lower = jnp.where(rim, 0.0, jnp.where(down_solid > 0.5, wall_down, lower))
                total = total + (jnp.where(up_solid > 0.5, wall_up, upper) - lower)
                base = [x - y for x, y in zip(v, q[n])]
                if n == 1:
                    held = (slot == (i & 7)) & top
                    shift = (i & 7) * 16
                else:
                    held = spot == i
                    shift = i
                for at, x in enumerate([*base, *q[t1], *q[t2], *inner_side, *aq[t1], *aq[t2]]):
                    x = pltpu.roll(x, shift, 1)
                    ref = first_j.at[at, i >> 3] if n == 1 else first_k.at[at]
                    pltpu.store(ref, x, mask=held)
            carry_sum[0] = total
            carry_sum[1] = wall_above
            return inner

        lax.fori_loop(0, EDGE, layer, 0)

        lefts = [full([carry_hi[s, at] for at in range(6)]) for s in range(4)]
        ghost = full(basic([raw_i[g, 1, c] for c in range(5)]))
        below, before, b1, b2 = join(EDGE, lefts, [ghost] * 4)
        total_ref[EDGE] = carry_sum[0] + dot([*before, *b1, *b2], below)

        def start(n, left, x):
            f = moments([full(basic(left))] * 4, [full(s) for s in quads(x[0:5], x[5:10], x[10:15])], n)
            return dot(x[15:30], f)

        start_k[...] = start(2, [kghost[g, 0, c] for c in range(5)], [first_k[at] for at in range(30)])
        found = start(
            1,
            [jnp.where(top, raw_j[g, c, 0], pltpu.roll(raw_j[g, c, 1], 4, 0)) for c in range(5)],
            [jnp.where(top, first_j[at, 0], pltpu.roll(first_j[at, 1], 4, 0)) for at in range(30)],
        )
        start_j[0] = found
        start_j[1] = pltpu.roll(found, 4, 0)

        def store(i, inner):
            turn = lax.rem(LANES - (i & 7) * 16, LANES)
            low_k = pltpu.roll(start_k[...], lax.rem(LANES - i, LANES), 1)
            low_j = pltpu.roll(start_j[i >> 3], turn, 1)
            x = total_ref[1 + i]
            x = x - jnp.where(spot == 0, low_k, 0.0) - jnp.where(zero_j, low_j, 0.0)
            found_ref[g, i] = jnp.where(solid[g, 1 + i] > 0.5, 0.0, 0.5 * jnp.abs(x))
            return inner

        lax.fori_loop(0, EDGE, store, 0)
        return carry

    lax.fori_loop(0, groups, group, 0)

    def write(i, carry):
        for g in range(groups):
            x = found_ref[g, i]
            for h in range(2):
                out_ref[
                    g * PACK : (g + 1) * PACK,
                    pl.ds(pl.multiple_of(i * PLANE + h * LANES, LANES), LANES),
                ] = x[h * PACK : (h + 1) * PACK]
        return carry

    lax.fori_loop(0, EDGE, write, 0)


def local(flow, adjoint, cut_flag, lateral_owner, lateral_link, vertical_link):
    blocks = flow.shape[0]
    groups = blocks // PACK
    peers = lax.axis_size("blk")
    capacity = max(2, 6 * blocks // peers)
    flow_t = jnp.transpose(flow, (1, 0, 2))
    adj_t = jnp.transpose(adjoint, (1, 0, 2))
    f32 = functools.partial(jax.ShapeDtypeStruct, dtype=jnp.float32)
    tile = functools.partial(pltpu.VMEM, dtype=jnp.float32)

    owner_t = jnp.transpose(lateral_owner, (1, 2, 0))
    link_t, ver_link_t = lateral_link.T, vertical_link.T
    rows = -(-capacity * 20 // 8) * 8
    received = (peers, rows, LANES)
    cells = (groups, 10, EDGE, 8, LANES)
    slopes = (groups, 3, 10, EDGE, 8, LANES)
    flags = (groups, EDGE, 8, LANES)
    kghosts = (groups, 2, 10, 8, LANES)
    edges = (groups, 2, 10, 2, 8, LANES)
    returned, packed, slope, solid, kghost, edge = pl.pallas_call(
        functools.partial(halo_kernel, capacity),
        out_shape=tuple(f32(s) for s in (received, cells, slopes, flags, kghosts, edges)),
        in_specs=[SMEM] * 3 + [HBM] * 3,
        out_specs=(HBM, HBM, HBM, HBM, VMEM, HBM),
        scratch_shapes=[
            tile((5, blocks, EDGE * PLANE)),
            tile((5, blocks, EDGE * PLANE)),
            pltpu.VMEM((blocks, EDGE * PLANE), jnp.int32),
            tile((4, 10, blocks, PLANE)),
            tile((2, 10, blocks, PLANE)),
            pltpu.VMEM((peers, 1, LANES), jnp.int32),
            pltpu.VMEM((peers, 1, LANES), jnp.int32),
            pltpu.SMEM((peers, 1, LANES), jnp.int32),
            tile(received),
            tile((10, blocks, PLANE)),
            tile((10, blocks, PLANE)),
            tile(cells),
            tile(slopes),
            tile(flags),
            tile(edges),
            *[pltpu.SemaphoreType.DMA((peers,))] * 4,
            pltpu.SemaphoreType.DMA((2,)),
            pltpu.SemaphoreType.DMA((2,)),
            pltpu.SemaphoreType.DMA,
            pltpu.SemaphoreType.DMA((3,)),
            pltpu.SemaphoreType.DMA((3 + groups,)),
        ],
        compiler_params=pltpu.CompilerParams(
            collective_id=0, has_side_effects=True, vmem_limit_bytes=63 * 1024 * 1024
        ),
        name="halo",
    )(owner_t, link_t, ver_link_t, flow_t, adj_t, cut_flag)

    return pl.pallas_call(
        main_kernel,
        out_shape=f32((blocks, EDGE * PLANE)),
        in_specs=[SMEM] * 2 + [HBM] * 6,
        out_specs=VMEM,
        scratch_shapes=[
            tile((peers * rows, LANES)),
            tile(kghosts),
            tile(cells),
            tile(slopes),
            tile((groups, EDGE + 2, 8, LANES)),
            tile(edges),
            pltpu.SemaphoreType.DMA((4 + 2 * groups,)),
            pltpu.SMEM((blocks * 4,), jnp.int32),
            pltpu.SMEM((peers,), jnp.int32),
            tile((groups, 2, 10, 8, LANES)),
            tile((groups, 10, 2, 8, LANES)),
            tile((10, 2, 8, LANES)),
            tile((6, 2, 8, LANES)),
            tile((6, 8, LANES)),
            tile((4, 6, 8, LANES)),
            tile((2, 8, LANES)),
            tile((30, 8, LANES)),
            tile((30, 2, 8, LANES)),
            tile((8, LANES)),
            tile((2, 8, LANES)),
            tile((EDGE + 1, 8, LANES)),
            tile(flags),
        ],
        compiler_params=pltpu.CompilerParams(vmem_limit_bytes=63 * 1024 * 1024),
        name="indicator",
    )(
        owner_t, link_t,
        returned.reshape(peers * rows, LANES), kghost, packed, slope, solid, edge,
    )


def solution(mesh):
    spec3 = P(("blk", "grp"), None, None)
    spec2 = P(("blk", "grp"), None)
    return jax.shard_map(
        local,
        mesh=mesh,
        in_specs=(spec3, spec3, spec2, spec3, spec2, spec2),
        out_specs=spec2,
        check_vma=False,
    )
```

time: 77.7 us -> 59.8 us (0.77)
  the two profiles are of different devices: /device:TPU:14 before, /device:TPU:0 now
where the time goes in v1:
time: 59.8 us; the launch traced here: 59.6 us
  Pallas kernels  59.6 us (100%)
    pallas_call x1, Pallas kernels, local(): pl.pallas_call(main_kernel, out_shape=f32((blocks, EDGE * PLANE)), in_spe...  30.7 us
    pallas_call x1, Pallas kernels, local(): pl.pallas_call(functools.partial(halo_kernel, capacity), out_shape=tuple(...  28.9 us

profile of v1, /device:TPU:0, one launch (start us, length us, event | category | flops | bytes accessed | tf_op | source)
XLA Modules:
  0.0 59.6 jit_solution(9070242709885283167)
XLA Ops:
  0.0 28.9 %halo.1 = (f32[8,184,128]{2,1,0:T(8,128)}, f32[3,10,16,8,128]{4,3,2,1,0:T(8,128)}, f32[3,3,10,16,8,128]{5,4,3,2,1,0:T(8,128)}, f32[3,16,8,128]{3,2,1,0:T(8,128)}...) custom-call(s32[4,1,12]{2,1,0:T(1,128)} %bitcast.9, s32[4,12]{1,0:T(4,128)} %bitcast.11, ...), custom_call_target="tpu_custom_call" | custom-call | tf_op jit(solution)/shard_map/halo/pallas_call | solution.py:761
  28.9 30.7 %indicator.1 = f32[12,4096]{1,0:T(8,128)} custom-call(s32[4,1,12]{2,1,0:T(1,128)} %bitcast.10, s32[4,12]{1,0:T(4,128)} %bitcast.12, f32[1472,128]{1,0:T(8,128)} %bitcast.8, f32[3,2,10,8,128]{4,3,2,1,0:T(8,128)} %get-tuple-element.12.kghost_hbm, f32[3,10,16,8,128]{4,3,2,1,0:T(8,128)} %get-tuple-element.13.val_hbm, ...), custom_call_target="tpu_custom_call" | custom-call | tf_op jit(solution)/shard_map/indicator/pallas_call | solution.py:795

commit v2 on v1

v2 whole, which is shorter than its diff:
```python
import functools

import jax
import jax.numpy as jnp
from jax import lax
from jax.experimental import pallas as pl
from jax.experimental.pallas import tpu as pltpu
from jax.sharding import PartitionSpec as P

EDGE = 16
PLANE = EDGE * EDGE
LANES = 128
PACK = 4
FREESTREAM = (1.0, 0.0, 0.0, 0.3, 1.0)
VMEM = pl.BlockSpec(memory_space=pltpu.VMEM)
SMEM = pl.BlockSpec(memory_space=pltpu.SMEM)
HBM = pl.BlockSpec(memory_space=pltpu.HBM)
MESH = pl.DeviceIdType.MESH


def iota(shape, dim):
    return lax.broadcasted_iota(jnp.int32, shape, dim)


def primitive(state):
    density, mom, energy = state[0], state[1:4], state[4]
    root = lax.rsqrt(density)
    inverse = root * root
    vel = [m * inverse for m in mom]
    square = vel[0] * vel[0] + vel[1] * vel[1] + vel[2] * vel[2]
    return [density, *vel, 0.4 * (energy - 0.5 * density * square)]


def pack_cells(flow_ref, adj_ref, flag_ref, val_ref, solid_ref):
    blocks = flow_ref.shape[1]
    groups = blocks // PACK
    top = iota((8, LANES), 0) < PACK

    def pack(parts):
        tiles = []
        for g in range(groups):
            at = g * PACK % 8
            first, second = parts[g * PACK // 8]
            if first.shape[0] == PACK:
                tiles.append(jnp.concatenate([first, second], axis=0))
            elif at == 0:
                tiles.append(jnp.where(top, first, pltpu.roll(second, 4, 0)))
            else:
                tiles.append(jnp.where(top, pltpu.roll(first, 4, 0), second))
        return tiles

    def read(load, i):
        parts = []
        for start in range(0, blocks, 8):
            rows = slice(start, min(start + 8, blocks))
            parts.append(
                [load(rows, pl.ds(pl.multiple_of(i * PLANE + h * LANES, LANES), LANES)) for h in range(2)]
            )
        return pack(parts)

    def load_layer(i, carry):
        flow = [read(lambda r, s: flow_ref[c, r, s], i) for c in range(5)]
        for g in range(groups):
            for c, x in enumerate(primitive([f[g] for f in flow])):
                val_ref[g, c, i] = x
        for c in range(5):
            for g, x in enumerate(read(lambda r, s: adj_ref[c, r, s], i)):
                val_ref[g, 5 + c, i] = x
        for g, x in enumerate(read(lambda r, s: flag_ref[r, s], i)):
            solid_ref[g, i] = x.astype(jnp.float32)
        return carry

    lax.fori_loop(0, EDGE, load_layer, 0)


def minmod(a, b):
    return jnp.where(a * b > 0.0, jnp.where(jnp.abs(a) < jnp.abs(b), a, b), 0.0)


def basic(state):
    rho, u, v, w, p = state
    inv_root = lax.rsqrt(rho)
    root = rho * inv_root
    enth = (3.5 * p) * (inv_root * inv_root) + 0.5 * (u * u + v * v + w * w)
    return [root, u, v, w, p, enth]


def full(parts):
    root, u, v, w, p, enth = parts
    return (root, (u, v, w), p, enth, (root * u, root * v, root * w), root * enth)


def roe(left, right, n):
    root_l, vel_l, p_l, h_l, rv_l, rh_l = left
    root_r, vel_r, p_r, h_r, rv_r, rh_r = right
    r = lax.rsqrt(root_l + root_r)
    inv = r * r
    vel = [(a + b) * inv for a, b in zip(rv_l, rv_r)]
    enth = (rh_l + rh_r) * inv
    un = vel[n]
    c_sq = 0.4 * enth - 0.2 * (vel[0] * vel[0] + vel[1] * vel[1] + vel[2] * vel[2])
    inv_c = lax.rsqrt(c_sq)
    c = c_sq * inv_c
    speed = jnp.abs(un)
    mach = speed * inv_c
    t = 1.0 - mach
    z = jnp.maximum(0.2 - jnp.abs(t), 0.0)
    w = (1.25 * z) * z
    even = jnp.maximum(t, 0.0) + w
    odd = jnp.minimum(mach, 1.0) - w
    odd = jnp.where(un < 0.0, -odd, odd)
    dp = p_r - p_l
    a = dp * inv_c
    b = (root_l * root_r) * (vel_r[n] - vel_l[n])
    first = (even * a + odd * b) * inv
    second = c * (odd * a + even * b)
    m_l = root_l * (root_l * (vel_l[n] + speed) - first)
    m_r = root_r * (root_r * (vel_r[n] - speed) - first)
    out = [m_l + m_r] + [m_l * x + m_r * y for x, y in zip(vel_l, vel_r)]
    out[1 + n] = out[1 + n] + ((p_l + p_r) - second)
    out.append((m_l * h_l + m_r * h_r) + (speed * dp - second * un))
    return out


def quads(base, q1, q2):
    low = [b - q for b, q in zip(base, q1)]
    high = [b + q for b, q in zip(base, q1)]
    return [
        basic([b - q for b, q in zip(low, q2)]),
        basic([b + q for b, q in zip(low, q2)]),
        basic([b - q for b, q in zip(high, q2)]),
        basic([b + q for b, q in zip(high, q2)]),
    ]


def moments(lefts, rights, n):
    f = [roe(a, b, n) for a, b in zip(lefts, rights)]
    zero, first, second = [], [], []
    for c in range(5):
        low, high = f[0][c] + f[1][c], f[2][c] + f[3][c]
        zero.append(low + high)
        first.append(high - low)
        second.append((f[1][c] - f[0][c]) + (f[3][c] - f[2][c]))
    return zero + first + second


def dot(a, b):
    total = a[0] * b[0]
    for x, y in zip(a[1:], b[1:]):
        total = total + x * y
    return total


def whole_kernel(
    capacity, owner_ref, link_ref, ver_link_ref, flow_hbm, adj_hbm, flag_hbm, out_ref,
    flow_ref, adj_ref, flag_ref, lat_ref, ver_ref, req_ref, want_ref, index_ref, spot_ref, place_ref,
    stage, ret_ref, low_ref, high_ref,
    val, slope, solid_ref, kghost, cval, cslope,
    raw_i, raw_j, jedge, kedge, carry_hi, carry_sum, first_k, total_ref, found_ref,
    ask_sem, asked_sem, send_sem, recv_sem, up_sem, down_sem, own_sem, in_sem,
):
    blocks = flow_ref.shape[1]
    groups = blocks // PACK
    peers = req_ref.shape[0]
    rows = stage.shape[1]
    used = capacity * 20
    me = lax.axis_index("blk")
    region = lax.axis_index("grp")
    last = lax.axis_size("grp") - 1
    has_low, has_high = region > 0, region < last

    barrier = pltpu.get_barrier_semaphore()
    for d in range(1, peers):
        pl.semaphore_signal(
            barrier, inc=1, device_id={"blk": lax.rem(me + d, peers)}, device_id_type=MESH
        )
    for there, step in ((has_low, -1), (has_high, 1)):
        @pl.when(there)
        def _():
            pl.semaphore_signal(
                barrier, inc=1, device_id={"grp": region + step}, device_id_type=MESH
            )

    loads = [
        pltpu.make_async_copy(a, b, in_sem.at[at])
        for at, (a, b) in enumerate(((flow_hbm, flow_ref), (adj_hbm, adj_ref), (flag_hbm, flag_ref)))
    ]
    for load in loads:
        load.start()

    holder = iota((peers, LANES), 0)
    column = iota((peers, LANES), 1)

    def ask(b, carry):
        asked, count, placed = carry
        for f in range(4):
            code = link_ref[f, b] // 5 * 4 + (f ^ 1)
            match = holder == owner_ref[f, 0, b]
            asked = jnp.where(match & (column == count), code, asked)
            placed = jnp.where(match & (column == b * 4 + f), holder * rows + count * 20, placed)
            count = count + match.astype(jnp.int32)
        return asked, count, placed

    nobody = jnp.zeros((peers, LANES), jnp.int32)
    asked, _, placed = lax.fori_loop(0, blocks, ask, (nobody, nobody, nobody))
    for p in range(peers):
        req_ref[p] = asked[p : p + 1]
    spot_ref[...] = jnp.sum(placed, axis=0, keepdims=True)
    places = pltpu.make_async_copy(spot_ref, place_ref, in_sem.at[3])
    places.start()

    def request(d):
        peer = lax.rem(me + d, peers)
        return pltpu.make_async_remote_copy(
            src_ref=req_ref.at[peer],
            dst_ref=want_ref.at[me],
            send_sem=ask_sem.at[d],
            recv_sem=asked_sem.at[d],
            device_id={"blk": peer},
            device_id_type=MESH,
        )

    own = pltpu.make_async_copy(req_ref.at[me], want_ref.at[me], own_sem)
    own.start()
    lane = iota((blocks, LANES), 1)
    slot, spot = lane >> 4, lane & 15

    def layers(ref, c):
        def tile(i, half):
            return ref[c, :, i * PLANE + half * LANES : i * PLANE + (half + 1) * LANES]

        out = {}
        for half in range(2):
            out[0, half] = tile(0, half)
            out[1, half] = tile(EDGE - 1, half)
            low_j = high_j = low_k = high_k = jnp.zeros((blocks, LANES), jnp.float32)
            for i in range(EDGE):
                if i // 8 == half:
                    il = i % 8
                    low_j = jnp.where(slot == il, pltpu.roll(tile(i, 0), il * 16, 1), low_j)
                    high_j = jnp.where(
                        slot == il, pltpu.roll(tile(i, 1), (il * 16 + 16) % LANES, 1), high_j
                    )
                here = tile(i, half)
                low_k = jnp.where(spot == i, pltpu.roll(here, i, 1), low_k)
                high_k = jnp.where(spot == i, pltpu.roll(here, (LANES + i - 15) % LANES, 1), high_k)
            out[2, half], out[3, half], out[4, half], out[5, half] = low_j, high_j, low_k, high_k
        return out

    def put(face, half, c, value):
        where = slice(half * LANES, (half + 1) * LANES)
        if face < 4:
            lat_ref[face, c, :, where] = value
        else:
            ver_ref[face - 4, c, :, where] = value

    loads[0].wait()
    loads[1].wait()
    def split(c, carry):
        @pl.when(c == 2)
        def _():
            pl.semaphore_wait(
                barrier, peers - 1 + has_low.astype(jnp.int32) + has_high.astype(jnp.int32)
            )
            for d in range(1, peers):
                request(d).start()

        for (face, half), value in layers(flow_ref, c).items():
            put(face, half, c, value)
        for (face, half), value in layers(adj_ref, c).items():
            put(face, half, 5 + c, value)
        return carry

    lax.fori_loop(0, 5, split, 0)
    for half in range(2):
        where = slice(half * LANES, (half + 1) * LANES)
        for ref, count in ((ver_ref, 2), (lat_ref, 4)):
            for face in range(count):
                prim = primitive([ref[face, c, :, where] for c in range(5)])
                for c in range(1, 5):
                    ref[face, c, :, where] = prim[c]

    def vertical(source, target, sem, step):
        return pltpu.make_async_remote_copy(
            src_ref=ver_ref.at[source],
            dst_ref=target,
            send_sem=sem.at[0],
            recv_sem=sem.at[1],
            device_id={"grp": region + step},
            device_id_type=MESH,
        )

    upward = vertical(1, low_ref, up_sem, 1)
    downward = vertical(0, high_ref, down_sem, -1)

    @pl.when(has_high)
    def _():
        upward.start()

    @pl.when(has_low)
    def _():
        downward.start()

    loads[2].wait()
    pack_cells(flow_ref, adj_ref, flag_ref, val, solid_ref)

    own.wait()
    for d in range(1, peers):
        request(d).wait()
    indices = pltpu.make_async_copy(want_ref, index_ref, own_sem)
    indices.start()
    indices.wait()

    def copy(d):
        peer = lax.rem(me + d, peers)
        return pltpu.make_async_remote_copy(
            src_ref=stage.at[peer, pl.ds(0, used)],
            dst_ref=ret_ref.at[pl.ds(pl.multiple_of(me * rows, 8), used)],
            send_sem=send_sem.at[d],
            recv_sem=recv_sem.at[d],
            device_id={"blk": peer},
            device_id_type=MESH,
        )

    def gather(peer):
        def one(s, carry):
            code = index_ref[peer, 0, s]
            face, block = code & 3, code >> 2
            for c in range(10):
                x = lat_ref[face, c, pl.ds(block, 1), :]
                for h in range(2):
                    stage[peer, pl.ds(s * 20 + c * 2 + h, 1), :] = x[:, h * LANES : (h + 1) * LANES]
            return carry

        lax.fori_loop(0, capacity, one, 0)

    def send(t, carry):
        sign = 2 * lax.rem(t, 2) - 1
        d = peers // 2 + (t + 1) // 2 * sign
        gather(lax.rem(me + d, peers))
        copy(d).start()
        return carry

    lax.fori_loop(0, peers - 1, send, 0)
    gather(me)
    mine = pltpu.make_async_copy(
        stage.at[me, pl.ds(0, used)], ret_ref.at[pl.ds(pl.multiple_of(me * rows, 8), used)], own_sem
    )
    mine.start()

    def far(ref):
        for c in range(10):
            ref[c] = jnp.full(ref.shape[1:], FREESTREAM[c] if c < 5 else 0.0, jnp.float32)

    @pl.when(has_low)
    def _():
        downward.wait_send()
        upward.wait_recv()

    @pl.when(jnp.logical_not(has_low))
    def _():
        far(low_ref)

    @pl.when(has_high)
    def _():
        upward.wait_send()
        downward.wait_recv()

    @pl.when(jnp.logical_not(has_high))
    def _():
        far(high_ref)

    lane = iota((8, LANES), 1)
    row = iota((8, LANES), 0)
    top = row < PACK
    slot, spot = lane >> 4, lane & 15


    def load_vertical(b, carry):
        g, at = b // PACK, lax.rem(b, PACK)
        for f, ref in enumerate((low_ref, high_ref)):
            link = ver_link_ref[f, b]
            code, block = lax.rem(link, 5), link // 5
            halves = [jnp.where(code == 4, h, code & 1) == 1 for h in range(2)]
            for c in range(10):
                x = ref[c, pl.ds(block, 1), :]
                for h, upper in enumerate(halves):
                    y = jnp.where(upper, x[:, LANES:], x[:, :LANES])
                    kghost[g, f, c, pl.ds(h * PACK + at, 1), :] = y
        return carry

    lax.fori_loop(0, blocks, load_vertical, 0)

    def codes(one_of, g, faces):
        code = jnp.zeros((8, LANES), jnp.int32)
        for r in range(8):
            code = jnp.where(row == r, one_of(faces[r // PACK], g * PACK + r % PACK), code)
        return code

    def picks(code, half, at):
        quarter = ((4 * half + (at >> 1)) << 4) + ((code & 1) << 3) + (spot >> 1)
        return jnp.where(code == 4, at * 16 + spot, quarter)

    def pick(x, index):
        return jnp.take_along_axis(x, index, axis=1, mode="promise_in_bounds")

    def vertical_code(f, b):
        one = lax.rem(ver_link_ref[f, b], 5)
        return jnp.where(one == 4, 4, ((one & 1) << 1) + (one >> 1))

    def lateral_code(f, b):
        return lax.rem(link_ref[f, b], 5)

    def ready_vertical(g, carry):
        for f in range(2):
            index = picks(codes(vertical_code, g, (f, f)), row >> 2, slot)
            for c in range(10):
                kghost[g, f, c] = pick(kghost[g, f, c], index)
        return carry

    lax.fori_loop(0, groups, ready_vertical, 0)

    def next_k(x):
        return pltpu.roll(x, LANES - 1, 1)

    def prev_k(x):
        return pltpu.roll(x, 1, 1)

    def next_j(x, edge_x):
        y = pltpu.roll(x, LANES - 16, 1)
        z = pltpu.roll(y, 4, 0)
        if edge_x is not None:
            z = jnp.where(top, z, edge_x)
        return jnp.where(slot == 7, z, y)

    def prev_j(x):
        y = pltpu.roll(x, 16, 1)
        return jnp.where(slot == 0, pltpu.roll(y, 4, 0), y)

    def side(store, n, high):
        order = [(s, t) for s in range(2) for t in range(2)]
        return [store[tuple([*st[:n], high, *st[n:]])] for st in order]

    def children(v, q):
        part = {}
        for a in range(2):
            base = [x + y if a else x - y for x, y in zip(v, q[0])]
            for at, state in enumerate(quads(base, q[1], q[2])):
                part[a, at >> 1, at & 1] = state
        return part, {at: full(state) for at, state in part.items()}

    last_j = (slot == 7) & jnp.logical_not(top)
    zero_j = (slot == 0) & top
    rim_j = last_j | zero_j

    rim_index = jnp.where(top, spot & 7, (spot + 7) & 7) * 16

    def rim_of(i):
        return slot == jnp.where(top, i & 7, (i + 7) & 7)

    def early(g, carry):
        def slopes(i, inner):
            below, above = jnp.maximum(i - 1, 0), jnp.minimum(i + 1, EDGE - 1)
            turn = (i & 7) * 16
            held = rim_of(i)
            for c in range(10):
                x = val[g, c, i]
                at_k = pltpu.roll(kghost[g, 1, c], 15 - i, 1)
                up_k = jnp.where(spot == 15, at_k, next_k(x)) - x
                at_k = pltpu.roll(kghost[g, 0, c], lax.rem(LANES - i, LANES), 1)
                down_k = x - jnp.where(spot == 0, at_k, prev_k(x))
                up_j, down_j = next_j(x, None) - x, x - prev_j(x)
                found = [
                    0.25 * minmod(val[g, c, above] - x, x - val[g, c, below]),
                    0.25 * minmod(up_j, down_j),
                    0.25 * minmod(up_k, down_k),
                ]
                for d in range(3):
                    slope[g, d, c, i] = found[d]
                pltpu.store(cval.at[g, c, i >> 3], pltpu.roll(x, turn, 1), mask=held)
                for d, y in enumerate((found[0], jnp.where(top, up_j, down_j), found[2])):
                    pltpu.store(cslope.at[g, d, c, i >> 3], pltpu.roll(y, turn, 1), mask=held)
                for d, y in enumerate((x - found[2], found[0], found[1])):
                    pltpu.store(first_k.at[g, d, c], pltpu.roll(y, i, 1), mask=spot == i)
            return inner

        lax.fori_loop(0, EDGE, slopes, 0)
        return carry

    lax.fori_loop(0, groups, early, 0)

    def finish(d, carry):
        copy(d).wait()
        return carry

    lax.fori_loop(1, peers, finish, 0)
    mine.wait()
    places.wait()

    def load_lateral(b, carry):
        g, at = b // PACK, lax.rem(b, PACK)
        for f in range(4):
            code = lax.rem(link_ref[f, b], 5)
            base = place_ref[0, b * 4 + f]
            for h in range(2):
                from_row = base + jnp.where(code == 4, h, code >> 1)
                for c in range(10):
                    x = ret_ref[pl.ds(from_row + 2 * c, 1), :]
                    if f < 2:
                        raw_i[g, f, c, pl.ds(h * PACK + at, 1), :] = x
                    else:
                        raw_j[g, c, h, pl.ds((f - 2) * PACK + at, 1), :] = x
        return carry

    lax.fori_loop(0, blocks, load_lateral, 0)

    def group(g, carry):
        for f in range(2):
            index = picks(codes(lateral_code, g, (f, f)), row >> 2, slot)
            for c in range(10):
                raw_i[g, f, c] = pick(raw_i[g, f, c], index)
        code = codes(lateral_code, g, (2, 3))
        for p in range(2):
            index = picks(code, p, jnp.where(top, slot, (slot + 1) & 7))
            for c in range(10):
                raw_j[g, c, p] = pick(raw_j[g, c, p], index)
        for c in range(10):
            for p in range(2):
                own, ghost = cval[g, c, p], raw_j[g, c, p]
                other = jnp.where(top, own - ghost, ghost - own)
                cslope[g, 1, c, p] = 0.25 * minmod(cslope[g, 1, c, p], other)
            first, second = val[g, c, 0], val[g, c, 1]
            x = 0.25 * minmod(second - first, first - raw_i[g, 0, c])
            slope[g, 0, c, 0] = x
            pltpu.store(cslope.at[g, 0, c, 0], x, mask=rim_of(0))
            first, second = val[g, c, EDGE - 2], val[g, c, EDGE - 1]
            x = 0.25 * minmod(raw_i[g, 1, c] - second, second - first)
            slope[g, 0, c, EDGE - 1] = x
            x = pltpu.roll(x, LANES - 16, 1)
            pltpu.store(cslope.at[g, 0, c, 1], x, mask=rim_of(EDGE - 1))

        for c in range(10):
            x = jnp.where(spot == 0, slope[g, 0, c, 0], first_k[g, 1, c])
            first_k[g, 1, c] = jnp.where(spot == 15, pltpu.roll(slope[g, 0, c, EDGE - 1], 15, 1), x)
            parts = [pick(cslope[g, 1, c, p], rim_index) for p in range(2)]
            first_k[g, 2, c] = jnp.where(rim_j, jnp.where(spot < 8, *parts), first_k[g, 2, c])

        for p in range(2):
            for at, x in enumerate(basic([raw_j[g, c, p] for c in range(5)])):
                jedge[at, p] = x
        for at, x in enumerate(basic([kghost[g, 1, c] for c in range(5)])):
            kedge[at] = x
        for at, x in enumerate(basic([raw_i[g, 0, c] for c in range(5)])):
            for s in range(4):
                carry_hi[s, at] = x
        nothing = jnp.zeros((8, LANES), jnp.float32)
        for at in range(3):
            carry_sum[at] = nothing

        def join(at, lefts, rights):
            f = moments(lefts, rights, 0)
            below = jnp.maximum(at - 1, 0)
            outer = [val[g, 5 + c, below] + slope[g, 0, 5 + c, below] for c in range(5)]
            aq1 = [slope[g, 1, 5 + c, below] for c in range(5)]
            aq2 = [slope[g, 2, 5 + c, below] for c in range(5)]
            return f, outer, aq1, aq2

        def layer(i, inner):
            turn = lax.rem(LANES - (i & 7) * 16, LANES)
            compact = i >> 3
            v = [val[g, c, i] for c in range(5)]
            av = [val[g, 5 + c, i] for c in range(5)]
            q = [[slope[g, d, c, i] for c in range(5)] for d in range(3)]
            aq = [[slope[g, d, 5 + c, i] for c in range(5)] for d in range(3)]
            for c in range(5):
                q[1][c] = jnp.where(rim_j, pltpu.roll(cslope[g, 1, c, compact], turn, 1), q[1][c])
                aq[1][c] = jnp.where(rim_j, pltpu.roll(cslope[g, 1, 5 + c, compact], turn, 1), aq[1][c])
                slope[g, 1, 5 + c, i] = aq[1][c]
            part, child = children(v, q)
            own_solid = solid_ref[g, i]
            total = jnp.zeros((8, LANES), jnp.float32)
            wall_above = None
            for n in range(3):
                t1, t2 = [a for a in range(3) if a != n]
                f = [roe(a, b, n) for a, b in zip(side(child, n, 0), side(child, n, 1))]
                inside = [(f[0][c] + f[1][c]) + (f[2][c] + f[3][c]) for c in range(5)]
                total = total - 2.0 * dot(aq[n], inside)
                outer = [x + y for x, y in zip(av, aq[n])]
                inner_side = [x - y for x, y in zip(av, aq[n])]
                cross = aq[t1][1 + n] * q[t1][4] + aq[t2][1 + n] * q[t2][4]
                wall_up = 8.0 * (outer[1 + n] * (v[4] + q[n][4]) + cross)
                wall_down = 8.0 * (inner_side[1 + n] * (v[4] - q[n][4]) + cross)
                if n == 0:
                    lefts = [full([carry_hi[s, at] for at in range(6)]) for s in range(4)]
                    below, before, b1, b2 = join(i, lefts, side(child, 0, 0))
                    for s, state in enumerate(side(part, 0, 1)):
                        for at in range(6):
                            carry_hi[s, at] = state[at]
                    ahead = dot([*before, *b1, *b2], below)
                    total_ref[i] = carry_sum[0] + jnp.where(own_solid > 0.5, carry_sum[1], ahead)
                    lower = dot([*inner_side, *aq[1], *aq[2]], below)
                    total = total - jnp.where(carry_sum[2] > 0.5, wall_down, lower)
                    wall_above = wall_up
                    continue
                if n == 1:
                    rims = [pltpu.roll(jedge[at, i >> 3], turn, 1) for at in range(6)]
                    rights = [
                        full([next_j(x, rim) for x, rim in zip(state, rims)]) for state in side(part, 1, 0)
                    ]
                    above = moments(side(child, 1, 1), rights, 1)
                    below = [prev_j(x) for x in above]
                    up_solid = jnp.where(last_j, 0.0, next_j(own_solid, None))
                    down_solid = prev_j(own_solid)
                    rim = zero_j
                else:
                    rims = [pltpu.roll(kedge[at], 15 - i, 1) for at in range(6)]
                    rights = [
                        full([jnp.where(spot == 15, rim, next_k(x)) for x, rim in zip(state, rims)])
                        for state in side(part, 2, 0)
                    ]
                    above = moments(side(child, 2, 1), rights, 2)
                    below = [prev_k(x) for x in above]
                    up_solid = jnp.where(spot == 15, 0.0, next_k(own_solid))
                    down_solid = prev_k(own_solid)
                    rim = spot == 0
                upper = dot([*outer, *aq[t1], *aq[t2]], above)
                lower = dot([*inner_side, *aq[t1], *aq[t2]], below)
                lower = jnp.where(rim, 0.0, jnp.where(down_solid > 0.5, wall_down, lower))
                total = total + (jnp.where(up_solid > 0.5, wall_up, upper) - lower)
            carry_sum[0] = total
            carry_sum[1] = wall_above
            carry_sum[2] = own_solid
            return inner

        lax.fori_loop(0, EDGE, layer, 0)

        lefts = [full([carry_hi[s, at] for at in range(6)]) for s in range(4)]
        ghost = full(basic([raw_i[g, 1, c] for c in range(5)]))
        below, before, b1, b2 = join(EDGE, lefts, [ghost] * 4)
        total_ref[EDGE] = carry_sum[0] + dot([*before, *b1, *b2], below)

        def start(n, left, x):
            f = moments([full(basic(left))] * 4, [full(s) for s in quads(x[0:5], x[10:15], x[20:25])], n)
            return dot([*x[5:10], *x[15:20], *x[25:30]], f)

        def joined(x):
            return jnp.where(top, x[0], pltpu.roll(x[1], 4, 0))

        low_k = start(2, [kghost[g, 0, c] for c in range(5)], [first_k[g, d, c] for d in range(3) for c in range(10)])
        across = [[joined(cslope[g, d, c]) for c in range(10)] for d in range(3)]
        base = [joined(cval[g, c]) - across[1][c] for c in range(10)]
        found = start(1, [joined(raw_j[g, c]) for c in range(5)], base + across[0] + across[2])
        low_j = [found, pltpu.roll(found, 4, 0)]
        for i in range(EDGE):
            x = total_ref[1 + i] - jnp.where(spot == 0, pltpu.roll(low_k, (LANES - i) % LANES, 1), 0.0)
            x = x - jnp.where(zero_j, pltpu.roll(low_j[i >> 3], (LANES - (i & 7) * 16) % LANES, 1), 0.0)
            found_ref[g, i] = jnp.where(solid_ref[g, i] > 0.5, 0.0, 0.5 * jnp.abs(x))
        return carry

    lax.fori_loop(0, groups, group, 0)

    def write(i, carry):
        for g in range(groups):
            x = found_ref[g, i]
            for h in range(2):
                out_ref[
                    g * PACK : (g + 1) * PACK,
                    pl.ds(pl.multiple_of(i * PLANE + h * LANES, LANES), LANES),
                ] = x[h * PACK : (h + 1) * PACK]
        return carry

    lax.fori_loop(0, EDGE, write, 0)


def local(flow, adjoint, cut_flag, lateral_owner, lateral_link, vertical_link):
    blocks = flow.shape[0]
    groups = blocks // PACK
    peers = lax.axis_size("blk")
    capacity = max(2, 6 * blocks // peers)
    rows = -(-capacity * 20 // 8) * 8
    tile = functools.partial(pltpu.VMEM, dtype=jnp.float32)
    pair = (8, LANES)

    def numbers(space, *shape):
        return space(shape, jnp.int32)

    return pl.pallas_call(
        functools.partial(whole_kernel, capacity),
        out_shape=jax.ShapeDtypeStruct((blocks, EDGE * PLANE), jnp.float32),
        in_specs=[SMEM] * 3 + [HBM] * 3,
        out_specs=VMEM,
        scratch_shapes=[
            tile((5, blocks, EDGE * PLANE)),
            tile((5, blocks, EDGE * PLANE)),
            numbers(pltpu.VMEM, blocks, EDGE * PLANE),
            tile((4, 10, blocks, PLANE)),
            tile((2, 10, blocks, PLANE)),
            numbers(pltpu.VMEM, peers, 1, LANES),
            numbers(pltpu.VMEM, peers, 1, LANES),
            numbers(pltpu.SMEM, peers, 1, LANES),
            numbers(pltpu.VMEM, 1, LANES),
            numbers(pltpu.SMEM, 1, LANES),
            tile((peers, rows, LANES)),
            tile((peers * rows, LANES)),
            tile((10, blocks, PLANE)),
            tile((10, blocks, PLANE)),
            tile((groups, 10, EDGE, *pair)),
            tile((groups, 3, 10, EDGE, *pair)),
            tile((groups, EDGE, *pair)),
            tile((groups, 2, 10, *pair)),
            tile((groups, 10, 2, *pair)),
            tile((groups, 3, 10, 2, *pair)),
            tile((groups, 2, 10, *pair)),
            tile((groups, 10, 2, *pair)),
            tile((6, 2, *pair)),
            tile((6, *pair)),
            tile((4, 6, *pair)),
            tile((3, *pair)),
            tile((groups, 3, 10, *pair)),
            tile((EDGE + 1, *pair)),
            tile((groups, EDGE, *pair)),
            *[pltpu.SemaphoreType.DMA((peers,))] * 4,
            pltpu.SemaphoreType.DMA((2,)),
            pltpu.SemaphoreType.DMA((2,)),
            pltpu.SemaphoreType.DMA,
            pltpu.SemaphoreType.DMA((4,)),
        ],
        compiler_params=pltpu.CompilerParams(
            collective_id=0, has_side_effects=True, vmem_limit_bytes=63 * 1024 * 1024
        ),
        name="indicator",
    )(
        jnp.transpose(lateral_owner, (1, 2, 0)), lateral_link.T, vertical_link.T,
        jnp.transpose(flow, (1, 0, 2)), jnp.transpose(adjoint, (1, 0, 2)), cut_flag,
    )


def solution(mesh):
    spec3 = P(("blk", "grp"), None, None)
    spec2 = P(("blk", "grp"), None)
    return jax.shard_map(
        local,
        mesh=mesh,
        in_specs=(spec3, spec3, spec2, spec3, spec2, spec2),
        out_specs=spec2,
        check_vma=False,
    )
```

time: 59.8 us -> 55.1 us (0.921)
  Pallas kernels: 59.6 us -> 53.2 us
  local copies, waits for them, and re-layouts: 0 us -> 1.67 us
    pallas_call x2 -> x1, Pallas kernels: 59.6 us -> 53.2 us  [local(): pl.pallas_call(functools.partial(whole_kernel, capacity), out_shape=jax.S...]
    unnamed x0 -> x1, local copies, waits for them, and re-layouts: none -> 1.67 us
where the time goes in v2:
time: 55.1 us; the launch traced here: 54.9 us
  Pallas kernels  53.2 us (97%)
  local copies, waits for them, and re-layouts  1.67 us (3%)
    pallas_call x1, Pallas kernels, local(): pl.pallas_call(functools.partial(whole_kernel, capacity), out_shape=jax.S...  53.2 us
    unnamed x1, local copies, waits for them, and re-layouts  1.67 us

profile of v2, /device:TPU:0, one launch (start us, length us, event | category | flops | bytes accessed | tf_op | source)
XLA Modules:
  0.0 54.9 jit_solution(6818378603432152521)
XLA Ops:
  0.0 53.2 %indicator.1 = f32[12,4096]{1,0:T(8,128)} custom-call(s32[4,1,12]{2,1,0:T(1,128)} %bitcast.7, s32[4,12]{1,0:T(4,128)} %bitcast.8, s32[2,12]{1,0:T(2,128)} %bitcast.9, f32[5,12,4096]{2,1,0:T(8,128)} %bitcast.5, f32[5,12,4096]{2,1,0:T(8,128)} %bitcast.6, s32[12,4096]{1,0:T(8,128)} %flag_hbm.1), custom_call_target="tpu_custom_call" | custom-call | tf_op jit(solution)/shard_map/indicator/pallas_call | solution.py:687
  53.2 1.7 %copy.8 = f32[12,4096]{1,0:T(8,128)} copy(f32[12,4096]{1,0:T(8,128)} %indicator.1) | data formatting | bytes 393216

commit v3 on v2

--- a/solution.py
+++ b/solution.py
@@ -107,7 +107,7 @@
     z = jnp.maximum(0.2 - jnp.abs(t), 0.0)
     w = (1.25 * z) * z
     even = jnp.maximum(t, 0.0) + w
-    odd = jnp.minimum(mach, 1.0) - w
+    odd = 1.0 - even
     odd = jnp.where(un < 0.0, -odd, odd)
     dp = p_r - p_l
     a = dp * inv_c
@@ -257,21 +257,20 @@
     loads[0].wait()
     loads[1].wait()
     def split(c, carry):
-        @pl.when(c == 2)
-        def _():
+        if c == 2:
             pl.semaphore_wait(
                 barrier, peers - 1 + has_low.astype(jnp.int32) + has_high.astype(jnp.int32)
             )
             for d in range(1, peers):
                 request(d).start()
-
         for (face, half), value in layers(flow_ref, c).items():
             put(face, half, c, value)
         for (face, half), value in layers(adj_ref, c).items():
             put(face, half, 5 + c, value)
         return carry
 
-    lax.fori_loop(0, 5, split, 0)
+    for c in range(5):
+        split(c, 0)
     for half in range(2):
         where = slice(half * LANES, (half + 1) * LANES)
         for ref, count in ((ver_ref, 2), (lat_ref, 4)):
@@ -632,7 +631,7 @@
             carry_sum[2] = own_solid
             return inner
 
-        lax.fori_loop(0, EDGE, layer, 0)
+        lax.fori_loop(0, EDGE, layer, 0, unroll=2)
 
         lefts = [full([carry_hi[s, at] for at in range(6)]) for s in range(4)]
         ghost = full(basic([raw_i[g, 1, c] for c in range(5)]))

time: 55.1 us -> 52.8 us (0.958)
  Pallas kernels: 53.2 us -> 50.9 us
    pallas_call x1, Pallas kernels: 53.2 us -> 50.9 us  [local(): pl.pallas_call(functools.partial(whole_kernel, capacity), out_shape=jax.S...]
where the time goes in v3:
time: 52.8 us; the launch traced here: 52.6 us
  Pallas kernels  50.9 us (96%)
  local copies, waits for them, and re-layouts  1.67 us (3%)
    pallas_call x1, Pallas kernels, local(): pl.pallas_call(functools.partial(whole_kernel, capacity), out_shape=jax.S...  50.9 us
    unnamed x1, local copies, waits for them, and re-layouts  1.67 us

profile of v3, /device:TPU:0, one launch (start us, length us, event | category | flops | bytes accessed | tf_op | source)
XLA Modules:
  0.0 52.6 jit_solution(280946802685230532)
XLA Ops:
  0.0 50.9 %indicator.1 = f32[12,4096]{1,0:T(8,128)} custom-call(s32[4,1,12]{2,1,0:T(1,128)} %bitcast.7, s32[4,12]{1,0:T(4,128)} %bitcast.8, s32[2,12]{1,0:T(2,128)} %bitcast.9, f32[5,12,4096]{2,1,0:T(8,128)} %bitcast.5, f32[5,12,4096]{2,1,0:T(8,128)} %bitcast.6, s32[12,4096]{1,0:T(8,128)} %flag_hbm.1), custom_call_target="tpu_custom_call" | custom-call | tf_op jit(solution)/shard_map/indicator/pallas_call | solution.py:686
  50.9 1.7 %copy.8 = f32[12,4096]{1,0:T(8,128)} copy(f32[12,4096]{1,0:T(8,128)} %indicator.1) | data formatting | bytes 393216

commit v4 on v3

--- a/solution.py
+++ b/solution.py
@@ -70,7 +70,7 @@
             solid_ref[g, i] = x.astype(jnp.float32)
         return carry
 
-    lax.fori_loop(0, EDGE, load_layer, 0)
+    lax.fori_loop(0, EDGE, load_layer, 0, unroll=2)
 
 
 def minmod(a, b):
@@ -331,7 +331,7 @@
                     stage[peer, pl.ds(s * 20 + c * 2 + h, 1), :] = x[:, h * LANES : (h + 1) * LANES]
             return carry
 
-        lax.fori_loop(0, capacity, one, 0)
+        lax.fori_loop(0, capacity, one, 0, unroll=min(3, capacity))
 
     def send(t, carry):
         sign = 2 * lax.rem(t, 2) - 1
@@ -388,7 +388,7 @@
                     kghost[g, f, c, pl.ds(h * PACK + at, 1), :] = y
         return carry
 
-    lax.fori_loop(0, blocks, load_vertical, 0)
+    lax.fori_loop(0, blocks, load_vertical, 0, unroll=2)
 
     def codes(one_of, g, faces):
         code = jnp.zeros((8, LANES), jnp.int32)
@@ -511,7 +511,7 @@
                         raw_j[g, c, h, pl.ds((f - 2) * PACK + at, 1), :] = x
         return carry
 
-    lax.fori_loop(0, blocks, load_lateral, 0)
+    lax.fori_loop(0, blocks, load_lateral, 0, unroll=2)
 
     def group(g, carry):
         for f in range(2):
@@ -631,7 +631,7 @@
             carry_sum[2] = own_solid
             return inner
 
-        lax.fori_loop(0, EDGE, layer, 0, unroll=2)
+        lax.fori_loop(0, EDGE, layer, 0, unroll=4)
 
         lefts = [full([carry_hi[s, at] for at in range(6)]) for s in range(4)]
         ghost = full(basic([raw_i[g, 1, c] for c in range(5)]))
@@ -668,7 +668,7 @@
                 ] = x[h * PACK : (h + 1) * PACK]
         return carry
 
-    lax.fori_loop(0, EDGE, write, 0)
+    lax.fori_loop(0, EDGE, write, 0, unroll=4)
 
 
 def local(flow, adjoint, cut_flag, lateral_owner, lateral_link, vertical_link):

time: 52.8 us -> 52.1 us (0.987)
  Pallas kernels: 50.9 us -> 50.3 us
    pallas_call x1, Pallas kernels: 50.9 us -> 50.3 us  [local(): pl.pallas_call(functools.partial(whole_kernel, capacity), out_shape=jax.S...]
where the time goes in v4:
time: 52.1 us; the launch traced here: 51.9 us
  Pallas kernels  50.3 us (97%)
  local copies, waits for them, and re-layouts  1.67 us (3%)
    pallas_call x1, Pallas kernels, local(): pl.pallas_call(functools.partial(whole_kernel, capacity), out_shape=jax.S...  50.3 us
    unnamed x1, local copies, waits for them, and re-layouts  1.67 us

profile of v4, /device:TPU:0, one launch (start us, length us, event | category | flops | bytes accessed | tf_op | source)
XLA Modules:
  0.0 51.9 jit_solution(5224083374728663912)
XLA Ops:
  0.0 50.3 %indicator.1 = f32[12,4096]{1,0:T(8,128)} custom-call(s32[4,1,12]{2,1,0:T(1,128)} %bitcast.7, s32[4,12]{1,0:T(4,128)} %bitcast.8, s32[2,12]{1,0:T(2,128)} %bitcast.9, f32[5,12,4096]{2,1,0:T(8,128)} %bitcast.5, f32[5,12,4096]{2,1,0:T(8,128)} %bitcast.6, s32[12,4096]{1,0:T(8,128)} %flag_hbm.1), custom_call_target="tpu_custom_call" | custom-call | tf_op jit(solution)/shard_map/indicator/pallas_call | solution.py:686
  50.3 1.7 %copy.8 = f32[12,4096]{1,0:T(8,128)} copy(f32[12,4096]{1,0:T(8,128)} %indicator.1) | data formatting | bytes 393216

commit v5 on v4

--- a/solution.py
+++ b/solution.py
@@ -88,6 +88,15 @@
 def full(parts):
     root, u, v, w, p, enth = parts
     return (root, (u, v, w), p, enth, (root * u, root * v, root * w), root * enth)
+
+
+def flat(state):
+    root, vel, p, enth, rv, rh = state
+    return [root, *vel, p, enth, *rv, rh]
+
+
+def unflat(x):
+    return (x[0], tuple(x[1:4]), x[4], x[5], tuple(x[6:9]), x[9])
 
 
 def roe(left, right, n):
@@ -549,7 +558,7 @@
                 jedge[at, p] = x
         for at, x in enumerate(basic([kghost[g, 1, c] for c in range(5)])):
             kedge[at] = x
-        for at, x in enumerate(basic([raw_i[g, 0, c] for c in range(5)])):
+        for at, x in enumerate(flat(full(basic([raw_i[g, 0, c] for c in range(5)])))):
             for s in range(4):
                 carry_hi[s, at] = x
         nothing = jnp.zeros((8, LANES), jnp.float32)
@@ -590,11 +599,11 @@
                 wall_up = 8.0 * (outer[1 + n] * (v[4] + q[n][4]) + cross)
                 wall_down = 8.0 * (inner_side[1 + n] * (v[4] - q[n][4]) + cross)
                 if n == 0:
-                    lefts = [full([carry_hi[s, at] for at in range(6)]) for s in range(4)]
+                    lefts = [unflat([carry_hi[s, at] for at in range(10)]) for s in range(4)]
                     below, before, b1, b2 = join(i, lefts, side(child, 0, 0))
-                    for s, state in enumerate(side(part, 0, 1)):
-                        for at in range(6):
-                            carry_hi[s, at] = state[at]
+                    for s, state in enumerate(side(child, 0, 1)):
+                        for at, x in enumerate(flat(state)):
+                            carry_hi[s, at] = x
                     ahead = dot([*before, *b1, *b2], below)
                     total_ref[i] = carry_sum[0] + jnp.where(own_solid > 0.5, carry_sum[1], ahead)
                     lower = dot([*inner_side, *aq[1], *aq[2]], below)
@@ -633,7 +642,7 @@
 
         lax.fori_loop(0, EDGE, layer, 0, unroll=4)
 
-        lefts = [full([carry_hi[s, at] for at in range(6)]) for s in range(4)]
+        lefts = [unflat([carry_hi[s, at] for at in range(10)]) for s in range(4)]
         ghost = full(basic([raw_i[g, 1, c] for c in range(5)]))
         below, before, b1, b2 = join(EDGE, lefts, [ghost] * 4)
         total_ref[EDGE] = carry_sum[0] + dot([*before, *b1, *b2], below)
@@ -713,7 +722,7 @@
             tile((groups, 10, 2, *pair)),
             tile((6, 2, *pair)),
             tile((6, *pair)),
-            tile((4, 6, *pair)),
+            tile((4, 10, *pair)),
             tile((3, *pair)),
             tile((groups, 3, 10, *pair)),
             tile((EDGE + 1, *pair)),

time: 52.1 us -> 52 us (level)
  no operation moved by 1% of the time
where the time goes in v5:
time: 52 us; the launch traced here: 51.8 us
  Pallas kernels  50.1 us (96%)
  local copies, waits for them, and re-layouts  1.67 us (3%)
    pallas_call x1, Pallas kernels, local(): pl.pallas_call(functools.partial(whole_kernel, capacity), out_shape=jax.S...  50.1 us
    unnamed x1, local copies, waits for them, and re-layouts  1.67 us

profile of v5, /device:TPU:0, one launch (start us, length us, event | category | flops | bytes accessed | tf_op | source)
XLA Modules:
  0.0 51.8 jit_solution(16585798645743992518)
XLA Ops:
  0.0 50.1 %indicator.1 = f32[12,4096]{1,0:T(8,128)} custom-call(s32[4,1,12]{2,1,0:T(1,128)} %bitcast.7, s32[4,12]{1,0:T(4,128)} %bitcast.8, s32[2,12]{1,0:T(2,128)} %bitcast.9, f32[5,12,4096]{2,1,0:T(8,128)} %bitcast.5, f32[5,12,4096]{2,1,0:T(8,128)} %bitcast.6, s32[12,4096]{1,0:T(8,128)} %flag_hbm.1), custom_call_target="tpu_custom_call" | custom-call | tf_op jit(solution)/shard_map/indicator/pallas_call | solution.py:695
  50.1 1.7 %copy.8 = f32[12,4096]{1,0:T(8,128)} copy(f32[12,4096]{1,0:T(8,128)} %indicator.1) | data formatting | bytes 393216
